TPU v7x, 1024 devices: a whole 8x8x8 slice. The times are simulated.
1024 devices in a mesh: lon: 32 (over z_hi, y), lat: 16 (over z_lo, x), rad: 2 (over core).
Axes of the slice: x: 8, y: 8, z: 8 (z_hi: 4, z_lo: 2; z = z_hi * 2 + z_lo), core: 2. Of those that a mesh axis runs over, the one named last changes fastest.
Arguments:
- adj_now: float32 [16, 512, 4096], P('rad', 'lat', 'lon'), may hold values from -6 to 6
- adj_next: float32 [16, 512, 4096], P('rad', 'lat', 'lon'), may hold values from -6 to 6
- fwd_now: float32 [16, 512, 4096], P('rad', 'lat', 'lon'), may hold values from -6 to 6
- fwd_next: float32 [16, 512, 4096], P('rad', 'lat', 'lon'), may hold values from -6 to 6
- stiffness: float32 [16, 512, 4096], P('rad', 'lat', 'lon'), may hold values from 0.04 to 0.15
- buoyancy: float32 [16, 512, 4096], P('rad', 'lat', 'lon'), may hold values from 0.6 to 1.5
- kernel_bulk_in: float32 [16, 512, 4096], P('rad', 'lat', 'lon'), may hold values from -6 to 6
- kernel_density_in: float32 [16, 512, 4096], P('rad', 'lat', 'lon'), may hold values from -6 to 6
Outputs:
- adj_out_now: float32 [16, 512, 4096], P('rad', 'lat', 'lon')
- adj_out_next: float32 [16, 512, 4096], P('rad', 'lat', 'lon')
- fwd_out_now: float32 [16, 512, 4096], P('rad', 'lat', 'lon')
- fwd_out_next: float32 [16, 512, 4096], P('rad', 'lat', 'lon')
- kernel_bulk: float32 [16, 512, 4096], P('rad', 'lat', 'lon')
- kernel_density: float32 [16, 512, 4096], P('rad', 'lat', 'lon')
All inputs are finite; a program needn't handle non-finite values.
Results may differ from a plain program's by a relative error of at most 0.00002.
Values sent between devices are 32-bit elements; how exact they have to be, the bound alone decides.
A program may use at most 32 MiB of HBM per device.

v0:
```python
import jax
import jax.numpy as jnp
from jax import lax
from jax.sharding import PartitionSpec as P

STEPS = 2


coef_near = 9.0 / 8.0
coef_far = -1.0 / 24.0


def padded_2(block, sides, width, periodic):
    for axis, dim in sides:
        count = lax.axis_size(axis)
        forward = [(i, i + 1) for i in range(count - 1)]
        if periodic:
            forward.append((count - 1, 0))
        backward = [(target, source) for source, target in forward]
        low = lax.ppermute(
            lax.slice_in_dim(block, block.shape[dim] - width, None, axis=dim), axis, forward
        )
        high = lax.ppermute(lax.slice_in_dim(block, 0, width, axis=dim), axis, backward)
        block = jnp.concatenate([low, block, high], axis=dim)
    return block


def piece(field, first, last, axis_num):
    return lax.slice_in_dim(field, first, last, axis=axis_num)


def rim_cells(stacked, width):
    wrapped_cells = padded_2(stacked, (("lon", 3),), width, True)
    return padded_2(wrapped_cells, (("lat", 2), ("rad", 1)), width, False)


def operate(adj_pad, fwd_pad, buoy_pad):
    lap_adj = None
    lap_fwd = None
    rho_term = None
    for dim_index in range(3):
        arrays = []
        for source in (adj_pad, fwd_pad, buoy_pad):
            for other in range(3):
                if other != dim_index:
                    source = piece(source, 3, source.shape[other] - 3, other)
            arrays.append(source)
        adj_part, fwd_part, buoy_part = arrays
        length = adj_part.shape[dim_index]

        def faces(field):
            near = piece(field, 2, length - 1, dim_index) - piece(field, 1, length - 2, dim_index)
            far = piece(field, 3, length, dim_index) - piece(field, 0, length - 3, dim_index)
            return coef_near * near + coef_far * far

        face_buoy = 0.5 * (
            piece(buoy_part, 1, length - 2, dim_index) + piece(buoy_part, 2, length - 1, dim_index)
        )
        grad_adj = faces(adj_part)
        grad_fwd = faces(fwd_part)
        count = length - 3

        def diverge(flux):
            near = piece(flux, 2, count - 1, dim_index) - piece(flux, 1, count - 2, dim_index)
            far = piece(flux, 3, count, dim_index) - piece(flux, 0, count - 3, dim_index)
            return coef_near * near + coef_far * far

        term_adj = diverge(face_buoy * grad_adj)
        term_fwd = diverge(face_buoy * grad_fwd)
        product = face_buoy * grad_adj * grad_fwd
        term_rho = 0.5 * (
            piece(product, 2, count - 1, dim_index) + piece(product, 1, count - 2, dim_index)
        )
        if lap_adj is None:
            lap_adj, lap_fwd, rho_term = (term_adj, term_fwd, term_rho)
        else:
            lap_adj = lap_adj + term_adj
            lap_fwd = lap_fwd + term_fwd
            rho_term = rho_term + term_rho
    return (lap_adj, lap_fwd, rho_term)


def shards(
    adj_now, adj_next, fwd_now, fwd_next, stiffness, buoyancy, kernel_bulk_in, kernel_density_in
):
    kernel_bulk = kernel_bulk_in
    kernel_density = kernel_density_in
    buoy_pad = rim_cells(buoyancy[None], 3)[0]
    for turn_index in range(STEPS):
        padded = rim_cells(jnp.stack([adj_now, fwd_now]), 3)
        lap_adj, lap_fwd, rho_term = operate(padded[0], padded[1], buoy_pad)
        kernel_bulk = kernel_bulk + adj_now * (stiffness * lap_fwd)
        kernel_density = kernel_density + rho_term
        new_adj = 2.0 * adj_now - adj_next + stiffness * lap_adj
        new_fwd = 2.0 * fwd_now - fwd_next + stiffness * lap_fwd
        adj_next, adj_now = (adj_now, new_adj)
        fwd_next, fwd_now = (fwd_now, new_fwd)
    return (adj_now, adj_next, fwd_now, fwd_next, kernel_bulk, kernel_density)


def solution(mesh):
    in_specs = (
        P("rad", "lat", "lon"),
        P("rad", "lat", "lon"),
        P("rad", "lat", "lon"),
        P("rad", "lat", "lon"),
        P("rad", "lat", "lon"),
        P("rad", "lat", "lon"),
        P("rad", "lat", "lon"),
        P("rad", "lat", "lon"),
    )
    out_specs = (
        P("rad", "lat", "lon"),
        P("rad", "lat", "lon"),
        P("rad", "lat", "lon"),
        P("rad", "lat", "lon"),
        P("rad", "lat", "lon"),
        P("rad", "lat", "lon"),
    )
    return jax.shard_map(shards, mesh=mesh, in_specs=in_specs, out_specs=out_specs, check_vma=False)
```

profile of v0, /device:TPU:7, one launch (start us, length us, event | category | flops | bytes accessed | tf_op | source)
XLA Modules:
  0.0 107.2 jit_solution(5019185009087147384)
XLA Ops:
  0.7 1.1 %fusion.129 = (f32[1,8,32,3]{3,2,1,0:T(8,128)S(1)}, f32[1,8,32,3]{3,2,1,0:T(8,128)S(1)}) fusion(f32[1,8,32,128]{3,2,1,0:T(8,128)} %bitcast.41), kind=kLoop, calls=%fused_computation.201 | loop fusion | bytes 12288 | tf_op jit(solution)/shard_map/slice | solution.py:21
  1.8 3.3 %collective-permute-start = (f32[1,8,32,3]{3,2,1,0:T(8,128)S(1)}, f32[1,8,32,3]{3,2,1,0:T(8,128)S(1)}, u32[]{:S(2)}, u32[]{:S(2)}) collective-permute-start(f32[1,8,32,3]{3,2,1,0:T(8,128)S(1)} %get-tuple-element.55), channel_id=1, source_target_pairs={{0,32},{32,64},{64,96},{96,128},{128,160},{160,192},{192,224},{224... | collective-permute-start | bytes 9224 | tf_op jit(solution)/shard_map/ppermute | solution.py:20
  5.1 18.4 %collective-permute-start.1 = (f32[1,8,32,3]{3,2,1,0:T(8,128)S(1)}, f32[1,8,32,3]{3,2,1,0:T(8,128)S(1)}, u32[]{:S(2)}, u32[]{:S(2)}) collective-permute-start(f32[1,8,32,3]{3,2,1,0:T(8,128)S(1)} %get-tuple-element.56), channel_id=1, source_target_pairs={{32,0},{64,32},{96,64},{128,96},{160,128},{192,160},{224,192},{256... | collective-permute-start | bytes 9224 | tf_op jit(solution)/shard_map/ppermute | solution.py:23
  23.5 1.2 %slice_maximum_fusion.1 = (f32[2,8,32,3]{3,2,1,0:T(8,128)S(1)}, f32[2,8,32,3]{3,2,1,0:T(8,128)S(1)}) fusion(f32[1,8,32,128]{3,2,1,0:T(8,128)} %bitcast.33, f32[1,8,32,128]{3,2,1,0:T(8,128)} %bitcast.25), kind=kLoop, calls=%fused_computation.41 | loop fusion | flops 3072 | bytes 274432 | tf_op jit(solution)/shard_map/stack | solution.py:90
  24.8 1.9 %collective-permute-start.6 = (f32[2,8,32,3]{3,2,1,0:T(8,128)S(1)}, f32[2,8,32,3]{3,2,1,0:T(8,128)S(1)}, u32[]{:S(2)}, u32[]{:S(2)}) collective-permute-start(f32[2,8,32,3]{3,2,1,0:T(8,128)S(1)} %get-tuple-element.53), channel_id=1, source_target_pairs={{0,32},{32,64},{64,96},{96,128},{128,160},{160,192},{192,224},{224... | collective-permute-start | bytes 18440 | tf_op jit(solution)/shard_map/ppermute | solution.py:20
  26.7 7.6 %collective-permute-start.7 = (f32[2,8,32,3]{3,2,1,0:T(8,128)S(1)}, f32[2,8,32,3]{3,2,1,0:T(8,128)S(1)}, u32[]{:S(2)}, u32[]{:S(2)}) collective-permute-start(f32[2,8,32,3]{3,2,1,0:T(8,128)S(1)} %get-tuple-element.54), channel_id=1, source_target_pairs={{32,0},{64,32},{96,64},{128,96},{160,128},{192,160},{224,192},{256... | collective-permute-start | bytes 18440 | tf_op jit(solution)/shard_map/ppermute | solution.py:23
  34.4 4.3 %collective-permute-start.2 = (f32[1,8,3,134]{3,2,1,0:T(4,128)S(1)}, f32[1,8,3,134]{3,2,1,0:T(4,128)S(1)}, u32[]{:S(2)}, u32[]{:S(2)}) collective-permute-start(f32[1,8,3,134]{3,2,1,0:T(4,128)S(1)} %get-tuple-element.47), channel_id=1, source_target_pairs={{0,2},{2,4},{4,6},{6,8},{8,10},{10,12},{12,14},{14,16},{16,18},{18... | collective-permute-start | bytes 38600 | tf_op jit(solution)/shard_map/ppermute | solution.py:20
  38.8 1.9 %collective-permute-start.3 = (f32[1,8,3,134]{3,2,1,0:T(4,128)S(1)}, f32[1,8,3,134]{3,2,1,0:T(4,128)S(1)}, u32[]{:S(2)}, u32[]{:S(2)}) collective-permute-start(f32[1,8,3,134]{3,2,1,0:T(4,128)S(1)} %get-tuple-element.48), channel_id=1, source_target_pairs={{2,0},{4,2},{6,4},{8,6},{10,8},{12,10},{14,12},{16,14},{18,16},{20... | collective-permute-start | bytes 38600 | tf_op jit(solution)/shard_map/ppermute | solution.py:23
  40.7 1.2 %collective-permute-done.6 = f32[2,8,32,3]{3,2,1,0:T(8,128)S(1)} collective-permute-done((f32[2,8,32,3]{3,2,1,0:T(8,128)S(1)}, f32[2,8,32,3]{3,2,1,0:T(8,128)S(1)}, u32[]{:S(2)}, u32[]{:S(2)}) %collective-permute-start.6) | collective-permute-done | bytes 6176 | tf_op jit(solution)/shard_map/ppermute | solution.py:20
  41.9 0.2 pad_maximum_fusion.14
  42.1 4.3 %collective-permute-start.8 = (f32[2,8,3,134]{3,2,1,0:T(4,128)S(1)}, f32[2,8,3,134]{3,2,1,0:T(4,128)S(1)}, u32[]{:S(2)}, u32[]{:S(2)}) collective-permute-start(f32[2,8,3,134]{3,2,1,0:T(4,128)S(1)} %get-tuple-element.37), channel_id=1, source_target_pairs={{0,2},{2,4},{4,6},{6,8},{8,10},{10,12},{12,14},{14,16},{16,18},{18... | collective-permute-start | bytes 77192 | tf_op jit(solution)/shard_map/ppermute | solution.py:20
  46.4 1.9 %collective-permute-start.9 = (f32[2,8,3,134]{3,2,1,0:T(4,128)S(1)}, f32[2,8,3,134]{3,2,1,0:T(4,128)S(1)}, u32[]{:S(2)}, u32[]{:S(2)}) collective-permute-start(f32[2,8,3,134]{3,2,1,0:T(4,128)S(1)} %get-tuple-element.38), channel_id=1, source_target_pairs={{2,0},{4,2},{6,4},{8,6},{10,8},{12,10},{14,12},{16,14},{18,16},{20... | collective-permute-start | bytes 77192 | tf_op jit(solution)/shard_map/ppermute | solution.py:23
  48.3 0.2 pad_maximum_fusion.4
  48.6 1.3 %collective-permute-start.4 = (f32[1,3,38,134]{3,2,1,0:T(8,128)S(1)}, f32[1,3,38,134]{3,2,1,0:T(8,128)S(1)}, u32[]{:S(2)}, u32[]{:S(2)}) collective-permute-start(f32[1,3,38,134]{3,2,1,0:T(8,128)S(1)} %get-tuple-element.49), channel_id=1, source_target_pairs={{0,1},{2,3},{4,5},{6,7},{8,9},{10,11},{12,13},{14,15},{16,17},{18,... | collective-permute-start | bytes 183320 | tf_op jit(solution)/shard_map/ppermute | solution.py:20
  49.9 5.7 %collective-permute-start.5 = (f32[1,3,38,134]{3,2,1,0:T(8,128)S(1)}, f32[1,3,38,134]{3,2,1,0:T(8,128)S(1)}, u32[]{:S(2)}, u32[]{:S(2)}) collective-permute-start(f32[1,3,38,134]{3,2,1,0:T(8,128)S(1)} %get-tuple-element.50), channel_id=1, source_target_pairs={{1,0},{3,2},{5,4},{7,6},{9,8},{11,10},{13,12},{15,14},{17,16},{19,... | collective-permute-start | bytes 183320 | tf_op jit(solution)/shard_map/ppermute | solution.py:23
  55.6 0.2 fusion.130
  55.9 0.3 pad_maximum_fusion.2
  56.2 0.5 fusion.107
  56.8 0.6 fusion.111
  57.4 1.3 %collective-permute-start.10 = (f32[2,3,38,134]{3,2,1,0:T(8,128)S(1)}, f32[2,3,38,134]{3,2,1,0:T(8,128)S(1)}, u32[]{:S(2)}, u32[]{:S(2)}) collective-permute-start(f32[2,3,38,134]{3,2,1,0:T(8,128)S(1)} %get-tuple-element.43), channel_id=1, source_target_pairs={{0,1},{2,3},{4,5},{6,7},{8,9},{10,11},{12,13},{14,15},{16,17},{18,... | collective-permute-start | bytes 366632 | tf_op jit(solution)/shard_map/ppermute | solution.py:20
  58.7 3.7 %collective-permute-start.11 = (f32[2,3,38,134]{3,2,1,0:T(8,128)S(1)}, f32[2,3,38,134]{3,2,1,0:T(8,128)S(1)}, u32[]{:S(2)}, u32[]{:S(2)}) collective-permute-start(f32[2,3,38,134]{3,2,1,0:T(8,128)S(1)} %get-tuple-element.44), channel_id=1, source_target_pairs={{1,0},{3,2},{5,4},{7,6},{9,8},{11,10},{13,12},{15,14},{17,16},{19,... | collective-permute-start | bytes 366632 | tf_op jit(solution)/shard_map/ppermute | solution.py:23
  62.5 0.2 maximum_bitcast_fusion
  62.7 0.8 collective-permute-done.11
  63.5 0.3 pad_maximum_fusion
  64.0 0.5 fusion.103
  64.6 0.3 copy-done.5
  64.9 0.2 fusion.94
  65.1 0.4 copy-done.7
  65.5 0.2 subtract_add_fusion.1
  65.7 0.1 slice_maximum_fusion
  65.8 1.9 %collective-permute-start.12 = (f32[2,8,32,3]{3,2,1,0:T(8,128)S(1)}, f32[2,8,32,3]{3,2,1,0:T(8,128)S(1)}, u32[]{:S(2)}, u32[]{:S(2)}) collective-permute-start(f32[2,8,32,3]{3,2,1,0:T(8,128)S(1)} %get-tuple-element.51), channel_id=1, source_target_pairs={{0,32},{32,64},{64,96},{96,128},{128,160},{160,192},{192,224},{224... | collective-permute-start | bytes 18440 | tf_op jit(solution)/shard_map/ppermute | solution.py:20
  67.7 7.8 %collective-permute-start.13 = (f32[2,8,32,3]{3,2,1,0:T(8,128)S(1)}, f32[2,8,32,3]{3,2,1,0:T(8,128)S(1)}, u32[]{:S(2)}, u32[]{:S(2)}) collective-permute-start(f32[2,8,32,3]{3,2,1,0:T(8,128)S(1)} %get-tuple-element.52), channel_id=1, source_target_pairs={{32,0},{64,32},{96,64},{128,96},{160,128},{192,160},{224,192},{256... | collective-permute-start | bytes 18440 | tf_op jit(solution)/shard_map/ppermute | solution.py:23
  75.6 9.5 %collective-permute-done.12 = f32[2,8,32,3]{3,2,1,0:T(8,128)S(1)} collective-permute-done((f32[2,8,32,3]{3,2,1,0:T(8,128)S(1)}, f32[2,8,32,3]{3,2,1,0:T(8,128)S(1)}, u32[]{:S(2)}, u32[]{:S(2)}) %collective-permute-start.12) | collective-permute-done | bytes 6176 | tf_op jit(solution)/shard_map/ppermute | solution.py:20
  85.1 0.2 pad_maximum_fusion.10
  85.3 4.2 %collective-permute-start.14 = (f32[2,8,3,134]{3,2,1,0:T(4,128)S(1)}, f32[2,8,3,134]{3,2,1,0:T(4,128)S(1)}, u32[]{:S(2)}, u32[]{:S(2)}) collective-permute-start(f32[2,8,3,134]{3,2,1,0:T(4,128)S(1)} %get-tuple-element.35), channel_id=1, source_target_pairs={{0,2},{2,4},{4,6},{6,8},{8,10},{10,12},{12,14},{14,16},{16,18},{18... | collective-permute-start | bytes 77192 | tf_op jit(solution)/shard_map/ppermute | solution.py:20
  89.5 1.9 %collective-permute-start.15 = (f32[2,8,3,134]{3,2,1,0:T(4,128)S(1)}, f32[2,8,3,134]{3,2,1,0:T(4,128)S(1)}, u32[]{:S(2)}, u32[]{:S(2)}) collective-permute-start(f32[2,8,3,134]{3,2,1,0:T(4,128)S(1)} %get-tuple-element.36), channel_id=1, source_target_pairs={{2,0},{4,2},{6,4},{8,6},{10,8},{12,10},{14,12},{16,14},{18,16},{20... | collective-permute-start | bytes 77192 | tf_op jit(solution)/shard_map/ppermute | solution.py:23
  91.5 4.3 %collective-permute-done.15 = f32[2,8,3,134]{3,2,1,0:T(4,128)S(1)} collective-permute-done((f32[2,8,3,134]{3,2,1,0:T(4,128)S(1)}, f32[2,8,3,134]{3,2,1,0:T(4,128)S(1)}, u32[]{:S(2)}, u32[]{:S(2)}) %collective-permute-start.15) | collective-permute-done | bytes 25760 | tf_op jit(solution)/shard_map/ppermute | solution.py:23
  95.7 0.3 pad_maximum_fusion.3
  96.2 1.3 %collective-permute-start.16 = (f32[2,3,38,134]{3,2,1,0:T(8,128)S(1)}, f32[2,3,38,134]{3,2,1,0:T(8,128)S(1)}, u32[]{:S(2)}, u32[]{:S(2)}) collective-permute-start(f32[2,3,38,134]{3,2,1,0:T(8,128)S(1)} %get-tuple-element.39), channel_id=1, source_target_pairs={{0,1},{2,3},{4,5},{6,7},{8,9},{10,11},{12,13},{14,15},{16,17},{18,... | collective-permute-start | bytes 366632 | tf_op jit(solution)/shard_map/ppermute | solution.py:20
  97.5 5.0 %collective-permute-start.17 = (f32[2,3,38,134]{3,2,1,0:T(8,128)S(1)}, f32[2,3,38,134]{3,2,1,0:T(8,128)S(1)}, u32[]{:S(2)}, u32[]{:S(2)}) collective-permute-start(f32[2,3,38,134]{3,2,1,0:T(8,128)S(1)} %get-tuple-element.40), channel_id=1, source_target_pairs={{1,0},{3,2},{5,4},{7,6},{9,8},{11,10},{13,12},{15,14},{17,16},{19,... | collective-permute-start | bytes 366632 | tf_op jit(solution)/shard_map/ppermute | solution.py:23
  102.5 0.5 fusion.121
  103.0 0.4 fusion.118
  103.5 0.1 collective-permute-done.17
  103.6 0.3 pad_maximum_fusion.1
  104.0 0.4 fusion.115
  104.5 0.8 fusion.69
  105.4 0.8 multiply_add_fusion
  106.3 0.9 fusion.47
  (45 shorter events, 0.9 us)
Async XLA Ops:
  0.6 33.7 %copy-start.4 = (f32[8,32,128]{2,1,0:T(8,128)S(1)}, f32[8,32,128]{2,1,0:T(8,128)}, u32[]{:S(2)}) copy-start(f32[8,32,128]{2,1,0:T(8,128)} %param.13) | copy-start | bytes 393220
  0.6 41.2 %copy-start = (f32[8,32,128]{2,1,0:T(8,128)S(1)}, f32[8,32,128]{2,1,0:T(8,128)}, u32[]{:S(2)}) copy-start(f32[8,32,128]{2,1,0:T(8,128)} %param.8) | copy-start | bytes 393220
  0.7 41.2 %copy-start.2 = (f32[8,32,128]{2,1,0:T(8,128)S(1)}, f32[8,32,128]{2,1,0:T(8,128)}, u32[]{:S(2)}) copy-start(f32[8,32,128]{2,1,0:T(8,128)} %param.10) | copy-start | bytes 393220
  1.8 32.5 %collective-permute-start = (f32[1,8,32,3]{3,2,1,0:T(8,128)S(1)}, f32[1,8,32,3]{3,2,1,0:T(8,128)S(1)}, u32[]{:S(2)}, u32[]{:S(2)}) collective-permute-start(f32[1,8,32,3]{3,2,1,0:T(8,128)S(1)} %get-tuple-element.55), channel_id=1, source_target_pairs={{0,32},{32,64},{64,96},{96,128},{128,160},{160,192},{192,224},{224... | collective-permute-start | bytes 9224 | tf_op jit(solution)/shard_map/ppermute | solution.py:20
  5.1 29.2 %collective-permute-start.1 = (f32[1,8,32,3]{3,2,1,0:T(8,128)S(1)}, f32[1,8,32,3]{3,2,1,0:T(8,128)S(1)}, u32[]{:S(2)}, u32[]{:S(2)}) collective-permute-start(f32[1,8,32,3]{3,2,1,0:T(8,128)S(1)} %get-tuple-element.56), channel_id=1, source_target_pairs={{32,0},{64,32},{96,64},{128,96},{160,128},{192,160},{224,192},{256... | collective-permute-start | bytes 9224 | tf_op jit(solution)/shard_map/ppermute | solution.py:23
  24.8 17.1 %collective-permute-start.6 = (f32[2,8,32,3]{3,2,1,0:T(8,128)S(1)}, f32[2,8,32,3]{3,2,1,0:T(8,128)S(1)}, u32[]{:S(2)}, u32[]{:S(2)}) collective-permute-start(f32[2,8,32,3]{3,2,1,0:T(8,128)S(1)} %get-tuple-element.53), channel_id=1, source_target_pairs={{0,32},{32,64},{64,96},{96,128},{128,160},{160,192},{192,224},{224... | collective-permute-start | bytes 18440 | tf_op jit(solution)/shard_map/ppermute | solution.py:20
  26.7 15.2 %collective-permute-start.7 = (f32[2,8,32,3]{3,2,1,0:T(8,128)S(1)}, f32[2,8,32,3]{3,2,1,0:T(8,128)S(1)}, u32[]{:S(2)}, u32[]{:S(2)}) collective-permute-start(f32[2,8,32,3]{3,2,1,0:T(8,128)S(1)} %get-tuple-element.54), channel_id=1, source_target_pairs={{32,0},{64,32},{96,64},{128,96},{160,128},{192,160},{224,192},{256... | collective-permute-start | bytes 18440 | tf_op jit(solution)/shard_map/ppermute | solution.py:23
  34.4 13.9 %collective-permute-start.2 = (f32[1,8,3,134]{3,2,1,0:T(4,128)S(1)}, f32[1,8,3,134]{3,2,1,0:T(4,128)S(1)}, u32[]{:S(2)}, u32[]{:S(2)}) collective-permute-start(f32[1,8,3,134]{3,2,1,0:T(4,128)S(1)} %get-tuple-element.47), channel_id=1, source_target_pairs={{0,2},{2,4},{4,6},{6,8},{8,10},{10,12},{12,14},{14,16},{16,18},{18... | collective-permute-start | bytes 38600 | tf_op jit(solution)/shard_map/ppermute | solution.py:20
  38.8 9.6 %collective-permute-start.3 = (f32[1,8,3,134]{3,2,1,0:T(4,128)S(1)}, f32[1,8,3,134]{3,2,1,0:T(4,128)S(1)}, u32[]{:S(2)}, u32[]{:S(2)}) collective-permute-start(f32[1,8,3,134]{3,2,1,0:T(4,128)S(1)} %get-tuple-element.48), channel_id=1, source_target_pairs={{2,0},{4,2},{6,4},{8,6},{10,8},{12,10},{14,12},{16,14},{18,16},{20... | collective-permute-start | bytes 38600 | tf_op jit(solution)/shard_map/ppermute | solution.py:23
  42.1 13.8 %collective-permute-start.8 = (f32[2,8,3,134]{3,2,1,0:T(4,128)S(1)}, f32[2,8,3,134]{3,2,1,0:T(4,128)S(1)}, u32[]{:S(2)}, u32[]{:S(2)}) collective-permute-start(f32[2,8,3,134]{3,2,1,0:T(4,128)S(1)} %get-tuple-element.37), channel_id=1, source_target_pairs={{0,2},{2,4},{4,6},{6,8},{8,10},{10,12},{12,14},{14,16},{16,18},{18... | collective-permute-start | bytes 77192 | tf_op jit(solution)/shard_map/ppermute | solution.py:20
  46.4 9.4 %collective-permute-start.9 = (f32[2,8,3,134]{3,2,1,0:T(4,128)S(1)}, f32[2,8,3,134]{3,2,1,0:T(4,128)S(1)}, u32[]{:S(2)}, u32[]{:S(2)}) collective-permute-start(f32[2,8,3,134]{3,2,1,0:T(4,128)S(1)} %get-tuple-element.38), channel_id=1, source_target_pairs={{2,0},{4,2},{6,4},{8,6},{10,8},{12,10},{14,12},{16,14},{18,16},{20... | collective-permute-start | bytes 77192 | tf_op jit(solution)/shard_map/ppermute | solution.py:23
  48.6 13.9 %collective-permute-start.4 = (f32[1,3,38,134]{3,2,1,0:T(8,128)S(1)}, f32[1,3,38,134]{3,2,1,0:T(8,128)S(1)}, u32[]{:S(2)}, u32[]{:S(2)}) collective-permute-start(f32[1,3,38,134]{3,2,1,0:T(8,128)S(1)} %get-tuple-element.49), channel_id=1, source_target_pairs={{0,1},{2,3},{4,5},{6,7},{8,9},{10,11},{12,13},{14,15},{16,17},{18,... | collective-permute-start | bytes 183320 | tf_op jit(solution)/shard_map/ppermute | solution.py:20
  49.9 12.6 %collective-permute-start.5 = (f32[1,3,38,134]{3,2,1,0:T(8,128)S(1)}, f32[1,3,38,134]{3,2,1,0:T(8,128)S(1)}, u32[]{:S(2)}, u32[]{:S(2)}) collective-permute-start(f32[1,3,38,134]{3,2,1,0:T(8,128)S(1)} %get-tuple-element.50), channel_id=1, source_target_pairs={{1,0},{3,2},{5,4},{7,6},{9,8},{11,10},{13,12},{15,14},{17,16},{19,... | collective-permute-start | bytes 183320 | tf_op jit(solution)/shard_map/ppermute | solution.py:23
  57.4 5.3 %collective-permute-start.10 = (f32[2,3,38,134]{3,2,1,0:T(8,128)S(1)}, f32[2,3,38,134]{3,2,1,0:T(8,128)S(1)}, u32[]{:S(2)}, u32[]{:S(2)}) collective-permute-start(f32[2,3,38,134]{3,2,1,0:T(8,128)S(1)} %get-tuple-element.43), channel_id=1, source_target_pairs={{0,1},{2,3},{4,5},{6,7},{8,9},{10,11},{12,13},{14,15},{16,17},{18,... | collective-permute-start | bytes 366632 | tf_op jit(solution)/shard_map/ppermute | solution.py:20
  58.7 4.8 %collective-permute-start.11 = (f32[2,3,38,134]{3,2,1,0:T(8,128)S(1)}, f32[2,3,38,134]{3,2,1,0:T(8,128)S(1)}, u32[]{:S(2)}, u32[]{:S(2)}) collective-permute-start(f32[2,3,38,134]{3,2,1,0:T(8,128)S(1)} %get-tuple-element.44), channel_id=1, source_target_pairs={{1,0},{3,2},{5,4},{7,6},{9,8},{11,10},{13,12},{15,14},{17,16},{19,... | collective-permute-start | bytes 366632 | tf_op jit(solution)/shard_map/ppermute | solution.py:23
  63.9 0.9 copy-start.5
  64.0 1.0 copy-start.6
  64.5 0.9 copy-start.7
  65.5 39.9 %copy-start.1 = (f32[8,32,128]{2,1,0:T(8,128)}, f32[8,32,128]{2,1,0:T(8,128)S(1)}, u32[]{:S(2)}) copy-start(f32[8,32,128]{2,1,0:T(8,128)S(1)} %fusion.94) | copy-start | bytes 393220
  65.7 40.6 %copy-start.3 = (f32[8,32,128]{2,1,0:T(8,128)}, f32[8,32,128]{2,1,0:T(8,128)S(1)}, u32[]{:S(2)}) copy-start(f32[8,32,128]{2,1,0:T(8,128)S(1)} %get-tuple-element.29) | copy-start | bytes 393220
  65.8 19.3 %collective-permute-start.12 = (f32[2,8,32,3]{3,2,1,0:T(8,128)S(1)}, f32[2,8,32,3]{3,2,1,0:T(8,128)S(1)}, u32[]{:S(2)}, u32[]{:S(2)}) collective-permute-start(f32[2,8,32,3]{3,2,1,0:T(8,128)S(1)} %get-tuple-element.51), channel_id=1, source_target_pairs={{0,32},{32,64},{64,96},{96,128},{128,160},{160,192},{192,224},{224... | collective-permute-start | bytes 18440 | tf_op jit(solution)/shard_map/ppermute | solution.py:20
  67.7 17.4 %collective-permute-start.13 = (f32[2,8,32,3]{3,2,1,0:T(8,128)S(1)}, f32[2,8,32,3]{3,2,1,0:T(8,128)S(1)}, u32[]{:S(2)}, u32[]{:S(2)}) collective-permute-start(f32[2,8,32,3]{3,2,1,0:T(8,128)S(1)} %get-tuple-element.52), channel_id=1, source_target_pairs={{32,0},{64,32},{96,64},{128,96},{160,128},{192,160},{224,192},{256... | collective-permute-start | bytes 18440 | tf_op jit(solution)/shard_map/ppermute | solution.py:23
  85.3 6.2 %collective-permute-start.14 = (f32[2,8,3,134]{3,2,1,0:T(4,128)S(1)}, f32[2,8,3,134]{3,2,1,0:T(4,128)S(1)}, u32[]{:S(2)}, u32[]{:S(2)}) collective-permute-start(f32[2,8,3,134]{3,2,1,0:T(4,128)S(1)} %get-tuple-element.35), channel_id=1, source_target_pairs={{0,2},{2,4},{4,6},{6,8},{8,10},{10,12},{12,14},{14,16},{16,18},{18... | collective-permute-start | bytes 77192 | tf_op jit(solution)/shard_map/ppermute | solution.py:20
  89.5 6.2 %collective-permute-start.15 = (f32[2,8,3,134]{3,2,1,0:T(4,128)S(1)}, f32[2,8,3,134]{3,2,1,0:T(4,128)S(1)}, u32[]{:S(2)}, u32[]{:S(2)}) collective-permute-start(f32[2,8,3,134]{3,2,1,0:T(4,128)S(1)} %get-tuple-element.36), channel_id=1, source_target_pairs={{2,0},{4,2},{6,4},{8,6},{10,8},{12,10},{14,12},{16,14},{18,16},{20... | collective-permute-start | bytes 77192 | tf_op jit(solution)/shard_map/ppermute | solution.py:23
  96.2 7.3 %collective-permute-start.16 = (f32[2,3,38,134]{3,2,1,0:T(8,128)S(1)}, f32[2,3,38,134]{3,2,1,0:T(8,128)S(1)}, u32[]{:S(2)}, u32[]{:S(2)}) collective-permute-start(f32[2,3,38,134]{3,2,1,0:T(8,128)S(1)} %get-tuple-element.39), channel_id=1, source_target_pairs={{0,1},{2,3},{4,5},{6,7},{8,9},{10,11},{12,13},{14,15},{16,17},{18,... | collective-permute-start | bytes 366632 | tf_op jit(solution)/shard_map/ppermute | solution.py:20
  97.5 6.1 %collective-permute-start.17 = (f32[2,3,38,134]{3,2,1,0:T(8,128)S(1)}, f32[2,3,38,134]{3,2,1,0:T(8,128)S(1)}, u32[]{:S(2)}, u32[]{:S(2)}) collective-permute-start(f32[2,3,38,134]{3,2,1,0:T(8,128)S(1)} %get-tuple-element.40), channel_id=1, source_target_pairs={{1,0},{3,2},{5,4},{7,6},{9,8},{11,10},{13,12},{15,14},{17,16},{19,... | collective-permute-start | bytes 366632 | tf_op jit(solution)/shard_map/ppermute | solution.py:23
  104.5 0.9 copy-start.8
  105.4 0.9 copy-start.9
where the time goes:
time: 108 us; the launch traced here: 107 us
  starting transfers between devices  77.9 us (72%)
  waiting for transfers between devices  15.9 us (15%)
  other arithmetic  9.82 us (9%)
  local copies, waits for them, and re-layouts  2.34 us (2%)
  between operations  1.14 us (1%)
    ppermute x9, starting transfers between devices, padded_2(): lax.ppermute(lax.slice_in_dim(block, 0, width, axis=dim), axis, backward)  54 us
    ppermute x9, starting transfers between devices, padded_2(): lax.ppermute(lax.slice_in_dim(block, block.shape[dim] - width, None, axis...  23.9 us
    ppermute x9, waiting for transfers between devices, padded_2(): lax.ppermute(lax.slice_in_dim(block, block.shape[dim] - width, None, axis...  10.7 us
    ppermute x9, waiting for transfers between devices, padded_2(): lax.ppermute(lax.slice_in_dim(block, 0, width, axis=dim), axis, backward)  5.22 us
    mul x6, other arithmetic, operate(): product = face_buoy * grad_adj * grad_fwd  3.01 us
  transfers between devices with their start and end apart: 18, of which 5 were waited for; matrix products, arithmetic and copies ran while one was open for 4% of the time, Pallas kernels for 0%

commit v1 on v0

v1 whole, which is shorter than its diff:
```python
import jax
import jax.numpy as jnp
from jax import lax
from jax.experimental import pallas as pl
from jax.experimental.pallas import tpu as pltpu
from jax.sharding import PartitionSpec as P

MESH = pl.DeviceIdType.MESH

near = 9.0 / 8.0
far = -1.0 / 24.0
half_near = near / 2
half_far = far / 2

LOW = 8
WIDE = 3


def kernel(
    nrad, nlat, nlon, counts,
    adj_now, adj_next, fwd_now, fwd_next, stiffness, buoyancy, bulk_in, density_in,
    out_adj_now, out_adj_next, out_fwd_now, out_fwd_next, out_bulk, out_density,
    first, second, side, total, flux, final,
    lon_send, lon_recv, lat_send, lat_recv,
    load_sem, save_sem, lon_ssem, lon_rsem, lat_ssem, lat_rsem, rad_ssem, rad_rsem,
):
    lons, lats, _ = counts
    lon = lax.axis_index("lon")
    lat = lax.axis_index("lat")
    core = lax.axis_index("rad")
    east = lax.rem(lon + 1, lons)
    west = lax.rem(lon + lons - 1, lons)
    other = 1 - core
    has_south = lat > 0
    has_north = lat < lats - 1

    barrier = pltpu.get_barrier_semaphore()

    def greet(where):
        pl.semaphore_signal(barrier, inc=1, device_id=where, device_id_type=MESH)

    greet({"lon": east})
    greet({"lon": west})
    greet({"rad": other})

    @pl.when(has_south)
    def _():
        greet({"lat": lat - 1})

    @pl.when(has_north)
    def _():
        greet({"lat": lat + 1})

    inside = (pl.ds(WIDE, nrad), pl.ds(LOW, nlat))
    sources = (adj_now, fwd_now, buoyancy, stiffness, adj_next, fwd_next, bulk_in, density_in)
    loads = []
    for k, source in enumerate(sources):
        target = first.at[(k,) + inside] if k < 3 else side.at[k - 3]
        loads.append(pltpu.make_async_copy(source, target, load_sem.at[k]))
        loads[-1].start()

    edge = 11 * core
    for block, fields in ((first, 3), (second, 2)):
        for f in range(fields):
            block[f, pl.ds(edge, WIDE)] = jnp.zeros((WIDE, nlat + 16, nlon), jnp.float32)

    @pl.when(jnp.logical_not(has_south))
    def _():
        for step in range(2):
            lat_recv[step, 0] = jnp.zeros(lat_recv.shape[2:], jnp.float32)

    @pl.when(jnp.logical_not(has_north))
    def _():
        for step in range(2):
            lat_recv[step, 1] = jnp.zeros(lat_recv.shape[2:], jnp.float32)

    lane = lax.broadcasted_iota(jnp.int32, (nlat, nlon), 1)
    group = lax.shift_right_logical(lane * 43, 7)

    def pack(block, fields, step):
        to_east = jnp.zeros((nlat, nlon), jnp.float32)
        to_west = jnp.zeros((nlat, nlon), jnp.float32)
        for f in range(fields):
            for r in range(nrad):
                n = f * nrad + r
                turned = pltpu.roll(block[f, WIDE + r, pl.ds(LOW, nlat)], (3 * n - 125) % 128, 1)
                to_east = jnp.where(group == n, turned, to_east)
                to_west = jnp.where(group == n + 1, turned, to_west)
                lat_send[step, 0, pl.ds(3 * n, 3)] = block[f, WIDE + r, pl.ds(LOW + nlat - 3, 3)]
                lat_send[step, 1, pl.ds(3 * n, 3)] = block[f, WIDE + r, pl.ds(LOW, 3)]
        lon_send[step, 0] = to_east
        lon_send[step, 1] = to_west

    def lon_copy(step, way, where):
        return pltpu.make_async_remote_copy(
            lon_send.at[step, way], lon_recv.at[step, way],
            lon_ssem.at[step, way], lon_rsem.at[step, way],
            device_id={"lon": where}, device_id_type=MESH,
        )

    def lat_copy(step, way, where, fields):
        rows = pl.ds(0, fields * nrad * 3)
        return pltpu.make_async_remote_copy(
            lat_send.at[step, way, rows], lat_recv.at[step, way, rows],
            lat_ssem.at[step, way], lat_rsem.at[step, way],
            device_id={"lat": where}, device_id_type=MESH,
        )

    def rad_copy(step, block):
        return pltpu.make_async_remote_copy(
            block.at[:, pl.ds(8 - 5 * core, WIDE), pl.ds(LOW, nlat)],
            block.at[:, pl.ds(11 * core, WIDE), pl.ds(LOW, nlat)],
            rad_ssem.at[step], rad_rsem.at[step],
            device_id={"rad": other}, device_id_type=MESH,
        )

    def send(step, block, fields):
        lon_copy(step, 0, east).start()
        lon_copy(step, 1, west).start()

        @pl.when(has_north)
        def _():
            lat_copy(step, 0, lat + 1, fields).start()

        @pl.when(has_south)
        def _():
            lat_copy(step, 1, lat - 1, fields).start()

        rad_copy(step, block).start()

    def wait_rad(step, block):
        rad_copy(step, block).wait_recv()

    def wait_lat(step, fields):
        @pl.when(has_south)
        def _():
            lat_copy(step, 0, lat - 1, fields).wait_recv()

        @pl.when(has_north)
        def _():
            lat_copy(step, 1, lat + 1, fields).wait_recv()

    def wait_lon(step):
        lon_copy(step, 0, west).wait_recv()
        lon_copy(step, 1, east).wait_recv()

    def wait_sent(step, block, fields):
        lon_copy(step, 0, east).wait_send()
        lon_copy(step, 1, west).wait_send()

        @pl.when(has_north)
        def _():
            lat_copy(step, 0, lat + 1, fields).wait_send()

        @pl.when(has_south)
        def _():
            lat_copy(step, 1, lat - 1, fields).wait_send()

        rad_copy(step, block).wait_send()

    def along_rad(block):
        for t in range(nlat // 8):
            rows = pl.ds(LOW + 8 * t, 8)
            adj, fwd, buoy = block[0, :, rows], block[1, :, rows], first[2, :, rows]

            def faces(p):
                return near * (p[2:13] - p[1:12]) + far * (p[3:14] - p[0:11])

            both = buoy[1:12] + buoy[2:13]
            grad_fwd = faces(fwd)
            flux_adj, flux_fwd = both * faces(adj), both * grad_fwd
            product = flux_adj * grad_fwd

            def diverge(q):
                return half_near * (q[2:10] - q[1:9]) + half_far * (q[3:11] - q[0:8])

            here = pl.ds(8 * t, 8)
            total[0, :, here] = diverge(flux_adj)
            total[1, :, here] = diverge(flux_fwd)
            total[2, :, here] = product[1:9] + product[2:10]

    def along_lat(step, block, fields):
        for f in range(fields):
            for r in range(nrad):
                n = f * nrad + r
                block[f, WIDE + r, pl.ds(LOW - 3, 3)] = lat_recv[step, 0, pl.ds(3 * n, 3)]
                block[f, WIDE + r, pl.ds(LOW + nlat, 3)] = lat_recv[step, 1, pl.ds(3 * n, 3)]
        rows = nlat + 8
        for r in range(nrad):
            def at(ref, f, k):
                return ref[f, WIDE + r, pl.ds(LOW - 2 + k, rows)]

            def faces(f):
                return near * (at(block, f, 1) - at(block, f, 0)) + far * (
                    at(block, f, 2) - at(block, f, -1)
                )

            both = at(first, 2, 0) + at(first, 2, 1)
            grad_fwd = faces(1)
            flux_adj = both * faces(0)
            flux[r, 0] = flux_adj
            flux[r, 1] = both * grad_fwd
            flux[r, 2] = flux_adj * grad_fwd

            def moved(f, k):
                return flux[r, f, pl.ds(2 + k, nlat)]

            for f in range(2):
                total[f, r] += half_near * (moved(f, 0) - moved(f, -1)) + half_far * (
                    moved(f, 1) - moved(f, -2)
                )
            total[2, r] += moved(2, 0) + moved(2, -1)

    def ahead(x, h, k):
        return pltpu.roll(jnp.where(lane < k, h, x), 128 - k, 1)

    def behind(x, h, k):
        return pltpu.roll(jnp.where(lane >= 128 - k, h, x), k, 1)

    def along_lon(step, block, r):
        def halo(at_step, f):
            turn = (125 - 3 * (f * nrad + r)) % 128
            return jnp.where(
                lane < 64,
                pltpu.roll(lon_recv[at_step, 1], turn, 1),
                pltpu.roll(lon_recv[at_step, 0], turn, 1),
            )

        def faces(x, h):
            return near * (ahead(x, h, 1) - x) + far * (ahead(x, h, 2) - behind(x, h, 1))

        def diverge(x, h):
            return half_near * (x - behind(x, h, 1)) + half_far * (
                ahead(x, h, 1) - behind(x, h, 2)
            )

        here = (WIDE + r, pl.ds(LOW, nlat))
        adj, fwd, buoy = block[(0,) + here], block[(1,) + here], first[(2,) + here]
        adj_h, fwd_h, buoy_h = halo(step, 0), halo(step, 1), halo(0, 2)
        both, both_h = buoy + ahead(buoy, buoy_h, 1), buoy_h + ahead(buoy_h, buoy, 1)
        grad, grad_h = faces(fwd, fwd_h), faces(fwd_h, fwd)
        q_adj, q_adj_h = both * faces(adj, adj_h), both_h * faces(adj_h, adj)
        q_fwd, q_fwd_h = both * grad, both_h * grad_h
        product, product_h = q_adj * grad, q_adj_h * grad_h
        lap_adj = stiff_ref[r] * (total[0, r] + diverge(q_adj, q_adj_h))
        lap_fwd = stiff_ref[r] * (total[1, r] + diverge(q_fwd, q_fwd_h))
        rho = total[2, r] + (product + behind(product, product_h, 1))
        return adj, fwd, lap_adj, lap_fwd, rho

    stiff_ref, adj_next_ref, fwd_next_ref, bulk_ref, density_ref = (side.at[k] for k in range(5))

    for k in range(3):
        loads[k].wait()
    pack(first, 3, 0)
    pl.semaphore_wait(barrier, 3 + has_south.astype(jnp.int32) + has_north.astype(jnp.int32))
    send(0, first, 3)
    for k in range(3, 8):
        loads[k].wait()

    wait_rad(0, first)
    along_rad(first)
    wait_lat(0, 3)
    along_lat(0, first, 3)
    wait_lon(0)
    for r in range(nrad):
        adj, fwd, lap_adj, lap_fwd, rho = along_lon(0, first, r)
        bulk_ref[r] += adj * lap_fwd
        density_ref[r] += 0.25 * rho
        second[0, WIDE + r, pl.ds(LOW, nlat)] = 2.0 * adj - adj_next_ref[r] + lap_adj
        second[1, WIDE + r, pl.ds(LOW, nlat)] = 2.0 * fwd - fwd_next_ref[r] + lap_fwd

    pack(second, 2, 1)
    send(1, second, 2)
    saves = [
        pltpu.make_async_copy(second.at[(0,) + inside], out_adj_next, save_sem.at[0]),
        pltpu.make_async_copy(second.at[(1,) + inside], out_fwd_next, save_sem.at[1]),
        pltpu.make_async_copy(final.at[0], out_adj_now, save_sem.at[2]),
        pltpu.make_async_copy(final.at[1], out_fwd_now, save_sem.at[3]),
        pltpu.make_async_copy(bulk_ref, out_bulk, save_sem.at[4]),
        pltpu.make_async_copy(density_ref, out_density, save_sem.at[5]),
    ]
    saves[0].start()
    saves[1].start()

    wait_rad(1, second)
    along_rad(second)
    wait_lat(1, 2)
    along_lat(1, second, 2)
    wait_lon(1)
    for r in range(nrad):
        adj, fwd, lap_adj, lap_fwd, rho = along_lon(1, second, r)
        bulk_ref[r] += adj * lap_fwd
        density_ref[r] += 0.25 * rho
        final[0, r] = 2.0 * adj - first[0, WIDE + r, pl.ds(LOW, nlat)] + lap_adj
        final[1, r] = 2.0 * fwd - first[1, WIDE + r, pl.ds(LOW, nlat)] + lap_fwd
    for save in saves[2:]:
        save.start()
    wait_sent(0, first, 3)
    wait_sent(1, second, 2)
    for save in saves:
        save.wait()


def solution(mesh):
    counts = (mesh.shape["lon"], mesh.shape["lat"], mesh.shape["rad"])

    def shards(*blocks):
        nrad, nlat, nlon = blocks[0].shape
        rows, f32, dma = nlat + 16, jnp.float32, pltpu.SemaphoreType.DMA
        return pl.pallas_call(
            lambda *refs: kernel(nrad, nlat, nlon, counts, *refs),
            out_shape=(jax.ShapeDtypeStruct(blocks[0].shape, f32),) * 6,
            in_specs=[pl.BlockSpec(memory_space=pl.ANY)] * 8,
            out_specs=(pl.BlockSpec(memory_space=pl.ANY),) * 6,
            scratch_shapes=[
                pltpu.VMEM((3, nrad + 2 * WIDE, rows, nlon), f32),
                pltpu.VMEM((2, nrad + 2 * WIDE, rows, nlon), f32),
                pltpu.VMEM((5, nrad, nlat, nlon), f32),
                pltpu.VMEM((3, nrad, nlat, nlon), f32),
                pltpu.VMEM((nrad, 3, nlat + 8, nlon), f32),
                pltpu.VMEM((2, nrad, nlat, nlon), f32),
                pltpu.VMEM((2, 2, nlat, nlon), f32),
                pltpu.VMEM((2, 2, nlat, nlon), f32),
                pltpu.VMEM((2, 2, 9 * nrad, nlon), f32),
                pltpu.VMEM((2, 2, 9 * nrad, nlon), f32),
                dma((8,)), dma((6,)),
                dma((2, 2)), dma((2, 2)), dma((2, 2)), dma((2, 2)), dma((2,)), dma((2,)),
            ],
            compiler_params=pltpu.CompilerParams(collective_id=0, has_side_effects=True),
            name="steps",
        )(*blocks)

    spec = P("rad", "lat", "lon")
    return jax.shard_map(
        shards, mesh=mesh, in_specs=(spec,) * 8, out_specs=(spec,) * 6, check_vma=False
    )
```

time: 108 us -> 40.7 us (0.38)
  the two profiles are of different devices: /device:TPU:7 before, /device:TPU:14 now
where the time goes in v1:
time: 40.7 us; the launch traced here: 40.4 us
  Pallas kernels  33.7 us (83%)
  local copies, waits for them, and re-layouts  6.06 us (15%)
  between operations  0.66 us (2%)
    pallas_call x1, Pallas kernels, shards(): pl.pallas_call(lambda *refs: kernel(nrad, nlat, nlon, counts, *refs), out...  33.7 us
    unnamed x16, local copies, waits for them, and re-layouts  6.06 us

profile of v1, /device:TPU:14, one launch (start us, length us, event | category | flops | bytes accessed | tf_op | source)
XLA Modules:
  0.0 40.4 jit_solution(1099229232198657901)
XLA Ops:
  0.6 33.7 %steps.1 = (f32[8,32,128]{2,1,0:T(8,128)}, f32[8,32,128]{2,1,0:T(8,128)}, f32[8,32,128]{2,1,0:T(8,128)}, f32[8,32,128]{2,1,0:T(8,128)}, f32[8,32,128]{2,1,0:T(8,128)}, /*index=5*/f32[8,32,128]{2,1,0:T(8,128)}) custom-call(f32[8,32,128]{2,1,0:T(8,128)} %refs_0_.1, f32[8,32,128]{2,1,0:T(8,128)} %refs_1_.1, f32[8,32,128]{2,1,0:T(8,128)} %refs_2_.1, ...), custom_call_target="tpu_custom_call" | custom-call | tf_op jit(solution)/shard_map/steps/pallas_call | solution.py:310
  34.4 0.0 copy-start.4
  34.4 1.6 %copy.20 = f32[8,32,128]{2,1,0:T(8,128)} copy(f32[8,32,128]{2,1,0:T(8,128)} %get-tuple-element.12) | data formatting | bytes 262144
  36.0 0.0 copy-done.4
  36.0 0.0 copy-start.3
  36.0 0.7 %copy.21 = f32[8,32,128]{2,1,0:T(8,128)} copy(f32[8,32,128]{2,1,0:T(8,128)S(1)} %copy-done.4) | data formatting | bytes 262144
  36.6 0.3 copy-done.3
  36.9 0.0 copy-start.2
  36.9 0.7 %copy.22 = f32[8,32,128]{2,1,0:T(8,128)} copy(f32[8,32,128]{2,1,0:T(8,128)S(1)} %copy-done.3) | data formatting | bytes 262144
  37.6 0.3 copy-done.2
  37.9 0.0 copy-start.1
  37.9 0.7 %copy.23 = f32[8,32,128]{2,1,0:T(8,128)} copy(f32[8,32,128]{2,1,0:T(8,128)S(1)} %copy-done.2) | data formatting | bytes 262144
  38.5 0.3 copy-done.1
  38.8 0.0 copy-start
  38.8 0.7 %copy.24 = f32[8,32,128]{2,1,0:T(8,128)} copy(f32[8,32,128]{2,1,0:T(8,128)S(1)} %copy-done.1) | data formatting | bytes 262144
  39.5 0.3 copy-done
  39.8 0.7 %copy.25 = f32[8,32,128]{2,1,0:T(8,128)} copy(f32[8,32,128]{2,1,0:T(8,128)S(1)} %copy-done) | data formatting | bytes 262144
Async XLA Ops:
  34.4 1.6 %copy-start.4 = (f32[8,32,128]{2,1,0:T(8,128)S(1)}, f32[8,32,128]{2,1,0:T(8,128)}, u32[]{:S(2)}) copy-start(f32[8,32,128]{2,1,0:T(8,128)} %get-tuple-element.13) | copy-start | bytes 393220
  36.0 1.0 %copy-start.3 = (f32[8,32,128]{2,1,0:T(8,128)S(1)}, f32[8,32,128]{2,1,0:T(8,128)}, u32[]{:S(2)}) copy-start(f32[8,32,128]{2,1,0:T(8,128)} %get-tuple-element.14) | copy-start | bytes 393220
  36.9 1.0 %copy-start.2 = (f32[8,32,128]{2,1,0:T(8,128)S(1)}, f32[8,32,128]{2,1,0:T(8,128)}, u32[]{:S(2)}) copy-start(f32[8,32,128]{2,1,0:T(8,128)} %get-tuple-element.15) | copy-start | bytes 393220
  37.9 1.0 %copy-start.1 = (f32[8,32,128]{2,1,0:T(8,128)S(1)}, f32[8,32,128]{2,1,0:T(8,128)}, u32[]{:S(2)}) copy-start(f32[8,32,128]{2,1,0:T(8,128)} %get-tuple-element.16) | copy-start | bytes 393220
  38.8 1.0 %copy-start = (f32[8,32,128]{2,1,0:T(8,128)S(1)}, f32[8,32,128]{2,1,0:T(8,128)}, u32[]{:S(2)}) copy-start(f32[8,32,128]{2,1,0:T(8,128)} %get-tuple-element.17) | copy-start | bytes 393220

commit v2 on v1

--- a/solution.py
+++ b/solution.py
@@ -20,9 +20,9 @@
     nrad, nlat, nlon, counts,
     adj_now, adj_next, fwd_now, fwd_next, stiffness, buoyancy, bulk_in, density_in,
     out_adj_now, out_adj_next, out_fwd_now, out_fwd_next, out_bulk, out_density,
-    first, second, side, total, flux, final,
+    first, second, side, total, flux,
     lon_send, lon_recv, lat_send, lat_recv,
-    load_sem, save_sem, lon_ssem, lon_rsem, lat_ssem, lat_rsem, rad_ssem, rad_rsem,
+    load_sem, lon_ssem, lon_rsem, lat_ssem, lat_rsem, rad_ssem, rad_rsem,
 ):
     lons, lats, _ = counts
     lon = lax.axis_index("lon")
@@ -227,24 +227,30 @@
             )
 
         def faces(x, h):
-            return near * (ahead(x, h, 1) - x) + far * (ahead(x, h, 2) - behind(x, h, 1))
-
-        def diverge(x, h):
-            return half_near * (x - behind(x, h, 1)) + half_far * (
-                ahead(x, h, 1) - behind(x, h, 2)
-            )
+            step, step_h = x - behind(x, h, 1), h - behind(h, x, 1)
+
+            def smooth(d, e):
+                return (near + far) * d + far * (ahead(d, e, 1) + behind(d, e, 1))
+
+            return smooth(step, step_h), smooth(step_h, step)
+
+        def diverge(q, h):
+            t, t_h = behind(q, h, 1), behind(h, q, 1)
+            v, v_h = half_near * t + half_far * q, half_near * t_h + half_far * h
+            return ahead(v, v_h, 2) - (half_far * t + half_near * q)
 
         here = (WIDE + r, pl.ds(LOW, nlat))
         adj, fwd, buoy = block[(0,) + here], block[(1,) + here], first[(2,) + here]
-        adj_h, fwd_h, buoy_h = halo(step, 0), halo(step, 1), halo(0, 2)
-        both, both_h = buoy + ahead(buoy, buoy_h, 1), buoy_h + ahead(buoy_h, buoy, 1)
-        grad, grad_h = faces(fwd, fwd_h), faces(fwd_h, fwd)
-        q_adj, q_adj_h = both * faces(adj, adj_h), both_h * faces(adj_h, adj)
+        buoy_h = halo(0, 2)
+        both, both_h = buoy + behind(buoy, buoy_h, 1), buoy_h + behind(buoy_h, buoy, 1)
+        grad, grad_h = faces(fwd, halo(step, 1))
+        slope, slope_h = faces(adj, halo(step, 0))
+        q_adj, q_adj_h = both * slope, both_h * slope_h
         q_fwd, q_fwd_h = both * grad, both_h * grad_h
         product, product_h = q_adj * grad, q_adj_h * grad_h
         lap_adj = stiff_ref[r] * (total[0, r] + diverge(q_adj, q_adj_h))
         lap_fwd = stiff_ref[r] * (total[1, r] + diverge(q_fwd, q_fwd_h))
-        rho = total[2, r] + (product + behind(product, product_h, 1))
+        rho = total[2, r] + (product + ahead(product, product_h, 1))
         return adj, fwd, lap_adj, lap_fwd, rho
 
     stiff_ref, adj_next_ref, fwd_next_ref, bulk_ref, density_ref = (side.at[k] for k in range(5))
@@ -271,16 +277,8 @@
 
     pack(second, 2, 1)
     send(1, second, 2)
-    saves = [
-        pltpu.make_async_copy(second.at[(0,) + inside], out_adj_next, save_sem.at[0]),
-        pltpu.make_async_copy(second.at[(1,) + inside], out_fwd_next, save_sem.at[1]),
-        pltpu.make_async_copy(final.at[0], out_adj_now, save_sem.at[2]),
-        pltpu.make_async_copy(final.at[1], out_fwd_now, save_sem.at[3]),
-        pltpu.make_async_copy(bulk_ref, out_bulk, save_sem.at[4]),
-        pltpu.make_async_copy(density_ref, out_density, save_sem.at[5]),
-    ]
-    saves[0].start()
-    saves[1].start()
+    out_adj_next[...] = second[(0,) + inside]
+    out_fwd_next[...] = second[(1,) + inside]
 
     wait_rad(1, second)
     along_rad(second)
@@ -289,16 +287,24 @@
     wait_lon(1)
     for r in range(nrad):
         adj, fwd, lap_adj, lap_fwd, rho = along_lon(1, second, r)
-        bulk_ref[r] += adj * lap_fwd
-        density_ref[r] += 0.25 * rho
-        final[0, r] = 2.0 * adj - first[0, WIDE + r, pl.ds(LOW, nlat)] + lap_adj
-        final[1, r] = 2.0 * fwd - first[1, WIDE + r, pl.ds(LOW, nlat)] + lap_fwd
-    for save in saves[2:]:
-        save.start()
+        out_bulk[r] = bulk_ref[r] + adj * lap_fwd
+        out_density[r] = density_ref[r] + 0.25 * rho
+        out_adj_now[r] = 2.0 * adj - first[0, WIDE + r, pl.ds(LOW, nlat)] + lap_adj
+        out_fwd_now[r] = 2.0 * fwd - first[1, WIDE + r, pl.ds(LOW, nlat)] + lap_fwd
     wait_sent(0, first, 3)
     wait_sent(1, second, 2)
-    for save in saves:
-        save.wait()
+
+
+def write_out(*refs):
+    results, outs, sems = refs[:6], refs[6:12], refs[12]
+    copies = [
+        pltpu.make_async_copy(result, out, sems.at[k])
+        for k, (result, out) in enumerate(zip(results, outs))
+    ]
+    for copy in copies:
+        copy.start()
+    for copy in copies:
+        copy.wait()
 
 
 def solution(mesh):
@@ -307,28 +313,35 @@
     def shards(*blocks):
         nrad, nlat, nlon = blocks[0].shape
         rows, f32, dma = nlat + 16, jnp.float32, pltpu.SemaphoreType.DMA
-        return pl.pallas_call(
+        held = pl.pallas_call(
             lambda *refs: kernel(nrad, nlat, nlon, counts, *refs),
-            out_shape=(jax.ShapeDtypeStruct(blocks[0].shape, f32),) * 6,
+            out_shape=(pltpu.VMEM(blocks[0].shape, f32),) * 6,
             in_specs=[pl.BlockSpec(memory_space=pl.ANY)] * 8,
-            out_specs=(pl.BlockSpec(memory_space=pl.ANY),) * 6,
+            out_specs=(pl.BlockSpec(memory_space=pltpu.VMEM),) * 6,
             scratch_shapes=[
                 pltpu.VMEM((3, nrad + 2 * WIDE, rows, nlon), f32),
                 pltpu.VMEM((2, nrad + 2 * WIDE, rows, nlon), f32),
                 pltpu.VMEM((5, nrad, nlat, nlon), f32),
                 pltpu.VMEM((3, nrad, nlat, nlon), f32),
                 pltpu.VMEM((nrad, 3, nlat + 8, nlon), f32),
-                pltpu.VMEM((2, nrad, nlat, nlon), f32),
                 pltpu.VMEM((2, 2, nlat, nlon), f32),
                 pltpu.VMEM((2, 2, nlat, nlon), f32),
                 pltpu.VMEM((2, 2, 9 * nrad, nlon), f32),
                 pltpu.VMEM((2, 2, 9 * nrad, nlon), f32),
-                dma((8,)), dma((6,)),
+                dma((8,)),
                 dma((2, 2)), dma((2, 2)), dma((2, 2)), dma((2, 2)), dma((2,)), dma((2,)),
             ],
             compiler_params=pltpu.CompilerParams(collective_id=0, has_side_effects=True),
             name="steps",
         )(*blocks)
+        return pl.pallas_call(
+            write_out,
+            out_shape=(jax.ShapeDtypeStruct(blocks[0].shape, f32),) * 6,
+            in_specs=[pl.BlockSpec(memory_space=pltpu.VMEM)] * 6,
+            out_specs=(pl.BlockSpec(memory_space=pl.ANY),) * 6,
+            scratch_shapes=[dma((6,))],
+            name="write_out",
+        )(*(pltpu.with_memory_space_constraint(x, pltpu.VMEM) for x in held))
 
     spec = P("rad", "lat", "lon")
     return jax.shard_map(

time: 40.7 us -> 38 us (0.934)
  local copies, waits for them, and re-layouts: 6.06 us -> 0 us
  Pallas kernels: 33.7 us -> 37.2 us
    unnamed x16 -> x0, local copies, waits for them, and re-layouts: 6.06 us -> none
    pallas_call x1, Pallas kernels: 33.7 us -> 36.3 us  [shards(): pl.pallas_call(lambda *refs: kernel(nrad, nlat, nlon, counts, *refs), out...]
    pallas_call x0 -> x1, Pallas kernels: none -> 0.93 us  [shards(): pl.pallas_call(write_out, out_shape=(jax.ShapeDtypeStruct(blocks[0].shape...]
where the time goes in v2:
time: 38 us; the launch traced here: 37.8 us
  Pallas kernels  37.2 us (98%)
  between operations  0.64 us (2%)
    pallas_call x1, Pallas kernels, shards(): pl.pallas_call(lambda *refs: kernel(nrad, nlat, nlon, counts, *refs), out...  36.3 us
    pallas_call x1, Pallas kernels, shards(): pl.pallas_call(write_out, out_shape=(jax.ShapeDtypeStruct(blocks[0].shape...  0.93 us

profile of v2, /device:TPU:14, one launch (start us, length us, event | category | flops | bytes accessed | tf_op | source)
XLA Modules:
  0.0 37.8 jit_solution(5351332305165021841)
XLA Ops:
  0.6 36.3 %steps.1 = (f32[8,32,128]{2,1,0:T(8,128)S(1)}, f32[8,32,128]{2,1,0:T(8,128)S(1)}, f32[8,32,128]{2,1,0:T(8,128)S(1)}, f32[8,32,128]{2,1,0:T(8,128)S(1)}, f32[8,32...) custom-call(f32[8,32,128]{2,1,0:T(8,128)} %refs_0_.1, f32[8,32,128]{2,1,0:T(8,128)} %refs_1_.1, f32[8,32,128]{2,1,0:T(8,128)} %refs_2_.1, ...), custom_call_target="tpu_custom_call" | custom-call | tf_op jit(solution)/shard_map/steps/pallas_call | solution.py:316
  36.9 0.9 %write_out.1 = (f32[8,32,128]{2,1,0:T(8,128)}, f32[8,32,128]{2,1,0:T(8,128)}, f32[8,32,128]{2,1,0:T(8,128)}, f32[8,32,128]{2,1,0:T(8,128)}, f32[8,32,128]{2,1,0:T(8,128)}, /*index=5*/f32[8,32,128]{2,1,0:T(8,128)}) custom-call(f32[8,32,128]{2,1,0:T(8,128)S(1)} %get-tuple-element.12.refs_0_, f32[8,32,128]{2,1,0:T(8,128)S(1)} %get-tuple-element.13.refs_1_, ...), custom_call_target="tpu_custom_call" | custom-call | tf_op jit(solution)/shard_map/write_out/pallas_call | solution.py:337

commit v3 on v2

--- a/solution.py
+++ b/solution.py
@@ -20,7 +20,7 @@
     nrad, nlat, nlon, counts,
     adj_now, adj_next, fwd_now, fwd_next, stiffness, buoyancy, bulk_in, density_in,
     out_adj_now, out_adj_next, out_fwd_now, out_fwd_next, out_bulk, out_density,
-    first, second, side, total, flux,
+    first, second, side, total, flux, lap, beyond, both, bands, bands_in,
     lon_send, lon_recv, lat_send, lat_recv,
     load_sem, lon_ssem, lon_rsem, lat_ssem, lat_rsem, rad_ssem, rad_rsem,
 ):
@@ -75,25 +75,30 @@
             lat_recv[step, 1] = jnp.zeros(lat_recv.shape[2:], jnp.float32)
 
     lane = lax.broadcasted_iota(jnp.int32, (nlat, nlon), 1)
-    group = lax.shift_right_logical(lane * 43, 7)
+    slot = lax.shift_right_logical(lane * 43, 8)
+    low_half = lane - 6 * slot < 3
 
     def pack(block, fields, step):
-        to_east = jnp.zeros((nlat, nlon), jnp.float32)
-        to_west = jnp.zeros((nlat, nlon), jnp.float32)
+        for first_field in range(0, fields, 2):
+            edges = jnp.zeros((nlat, nlon), jnp.float32)
+            for f in range(first_field, min(first_field + 2, fields)):
+                for r in range(nrad):
+                    n = (f - first_field) * nrad + r
+                    turned = pltpu.roll(
+                        block[f, WIDE + r, pl.ds(LOW, nlat)], (6 * n - 125) % 128, 1
+                    )
+                    edges = jnp.where(slot == n, turned, edges)
+            lon_send[step, first_field // 2] = edges
         for f in range(fields):
             for r in range(nrad):
                 n = f * nrad + r
-                turned = pltpu.roll(block[f, WIDE + r, pl.ds(LOW, nlat)], (3 * n - 125) % 128, 1)
-                to_east = jnp.where(group == n, turned, to_east)
-                to_west = jnp.where(group == n + 1, turned, to_west)
                 lat_send[step, 0, pl.ds(3 * n, 3)] = block[f, WIDE + r, pl.ds(LOW + nlat - 3, 3)]
                 lat_send[step, 1, pl.ds(3 * n, 3)] = block[f, WIDE + r, pl.ds(LOW, 3)]
-        lon_send[step, 0] = to_east
-        lon_send[step, 1] = to_west
 
     def lon_copy(step, way, where):
+        parts = pl.ds(0, 2 - step)
         return pltpu.make_async_remote_copy(
-            lon_send.at[step, way], lon_recv.at[step, way],
+            lon_send.at[step, parts], lon_recv.at[step, way, parts],
             lon_ssem.at[step, way], lon_rsem.at[step, way],
             device_id={"lon": where}, device_id_type=MESH,
         )
@@ -217,44 +222,72 @@
     def behind(x, h, k):
         return pltpu.roll(jnp.where(lane >= 128 - k, h, x), k, 1)
 
-    def along_lon(step, block, r):
-        def halo(at_step, f):
-            turn = (125 - 3 * (f * nrad + r)) % 128
-            return jnp.where(
-                lane < 64,
-                pltpu.roll(lon_recv[at_step, 1], turn, 1),
-                pltpu.roll(lon_recv[at_step, 0], turn, 1),
-            )
-
-        def faces(x, h):
-            step, step_h = x - behind(x, h, 1), h - behind(h, x, 1)
-
-            def smooth(d, e):
-                return (near + far) * d + far * (ahead(d, e, 1) + behind(d, e, 1))
-
-            return smooth(step, step_h), smooth(step_h, step)
-
-        def diverge(q, h):
-            t, t_h = behind(q, h, 1), behind(h, q, 1)
-            v, v_h = half_near * t + half_far * q, half_near * t_h + half_far * h
-            return ahead(v, v_h, 2) - (half_far * t + half_near * q)
-
+    def fetch_halos(step, fields):
+        for f in fields:
+            edges = jnp.where(low_half, lon_recv[step, 0, f // 2], lon_recv[step, 1, f // 2])
+            for r in range(nrad):
+                beyond[f, r] = pltpu.roll(edges, (125 - 6 * ((f % 2) * nrad + r)) % 128, 1)
+
+    ring = 2 * nlon
+
+    def banded(columns, start):
+        source = lax.broadcasted_iota(jnp.int32, (ring, columns), 0)
+        place = lax.broadcasted_iota(jnp.int32, (ring, columns), 1)
+        gap = lax.bitwise_and(source - place - start + ring, ring - 1)
+        out = jnp.where(gap == 1, 27.0, 0.0) - jnp.where(gap == 0, 27.0, 0.0)
+        out = out - jnp.where(gap == 2, 1.0, 0.0) + jnp.where(gap == ring - 1, 1.0, 0.0)
+        return out.astype(jnp.bfloat16)
+
+    def set_bands():
+        for k in range(3):
+            bands[pl.ds(ring * k, ring)] = banded(ring, 0)
+            bands_in[pl.ds(ring * k, ring)] = banded(nlon, -1)
+
+    def times(x, h, matrix):
+        parts = []
+        rest = (x, h)
+        for k in range(3):
+            cut = tuple(v.astype(jnp.bfloat16) for v in rest)
+            parts.extend(cut)
+            if k < 2:
+                rest = tuple(v - c.astype(jnp.float32) for v, c in zip(rest, cut))
+        return jnp.dot(
+            jnp.concatenate(parts, axis=1), matrix[...], preferred_element_type=jnp.float32
+        )
+
+    cells = nrad * nlat
+
+    def set_both():
+        for r in range(nrad):
+            buoy, buoy_h = first[2, WIDE + r, pl.ds(LOW, nlat)], beyond[2, r]
+            both[r, :, pl.ds(0, nlon)] = buoy + ahead(buoy, buoy_h, 1)
+            both[r, :, pl.ds(nlon, nlon)] = buoy_h + ahead(buoy_h, buoy, 1)
+
+    def along_lon(block):
+        weight = both[...].reshape(cells, ring)
+        slopes, fluxes = [], []
+        for f in range(2):
+            x = block[f, pl.ds(WIDE, nrad), pl.ds(LOW, nlat)].reshape(cells, nlon)
+            slope = times(x, beyond[f].reshape(cells, nlon), bands)
+            q = weight * slope
+            lap[f] = times(q[:, :nlon], q[:, nlon:], bands_in).reshape(nrad, nlat, nlon)
+            slopes.append(slope)
+            fluxes.append(q)
+        product = (fluxes[0] * slopes[1]).reshape(nrad, nlat, ring)
+        for r in range(nrad):
+            here, past = product[r, :, :nlon], product[r, :, nlon:]
+            lap[2, r] = here + behind(here, past, 1)
+
+    def close(block, r):
         here = (WIDE + r, pl.ds(LOW, nlat))
-        adj, fwd, buoy = block[(0,) + here], block[(1,) + here], first[(2,) + here]
-        buoy_h = halo(0, 2)
-        both, both_h = buoy + behind(buoy, buoy_h, 1), buoy_h + behind(buoy_h, buoy, 1)
-        grad, grad_h = faces(fwd, halo(step, 1))
-        slope, slope_h = faces(adj, halo(step, 0))
-        q_adj, q_adj_h = both * slope, both_h * slope_h
-        q_fwd, q_fwd_h = both * grad, both_h * grad_h
-        product, product_h = q_adj * grad, q_adj_h * grad_h
-        lap_adj = stiff_ref[r] * (total[0, r] + diverge(q_adj, q_adj_h))
-        lap_fwd = stiff_ref[r] * (total[1, r] + diverge(q_fwd, q_fwd_h))
-        rho = total[2, r] + (product + ahead(product, product_h, 1))
-        return adj, fwd, lap_adj, lap_fwd, rho
+        lap_adj = stiff_ref[r] * (total[0, r] + (1 / 1152) * lap[0, r])
+        lap_fwd = stiff_ref[r] * (total[1, r] + (1 / 1152) * lap[1, r])
+        rho = 0.25 * total[2, r] + (1 / 2304) * lap[2, r]
+        return block[(0,) + here], block[(1,) + here], lap_adj, lap_fwd, rho
 
     stiff_ref, adj_next_ref, fwd_next_ref, bulk_ref, density_ref = (side.at[k] for k in range(5))
 
+    set_bands()
     for k in range(3):
         loads[k].wait()
     pack(first, 3, 0)
@@ -268,10 +301,13 @@
     wait_lat(0, 3)
     along_lat(0, first, 3)
     wait_lon(0)
+    fetch_halos(0, range(3))
+    set_both()
+    along_lon(first)
     for r in range(nrad):
-        adj, fwd, lap_adj, lap_fwd, rho = along_lon(0, first, r)
+        adj, fwd, lap_adj, lap_fwd, rho = close(first, r)
         bulk_ref[r] += adj * lap_fwd
-        density_ref[r] += 0.25 * rho
+        density_ref[r] += rho
         second[0, WIDE + r, pl.ds(LOW, nlat)] = 2.0 * adj - adj_next_ref[r] + lap_adj
         second[1, WIDE + r, pl.ds(LOW, nlat)] = 2.0 * fwd - fwd_next_ref[r] + lap_fwd
 
@@ -285,10 +321,12 @@
     wait_lat(1, 2)
     along_lat(1, second, 2)
     wait_lon(1)
+    fetch_halos(1, range(2))
+    along_lon(second)
     for r in range(nrad):
-        adj, fwd, lap_adj, lap_fwd, rho = along_lon(1, second, r)
+        adj, fwd, lap_adj, lap_fwd, rho = close(second, r)
         out_bulk[r] = bulk_ref[r] + adj * lap_fwd
-        out_density[r] = density_ref[r] + 0.25 * rho
+        out_density[r] = density_ref[r] + rho
         out_adj_now[r] = 2.0 * adj - first[0, WIDE + r, pl.ds(LOW, nlat)] + lap_adj
         out_fwd_now[r] = 2.0 * fwd - first[1, WIDE + r, pl.ds(LOW, nlat)] + lap_fwd
     wait_sent(0, first, 3)
@@ -324,8 +362,13 @@
                 pltpu.VMEM((5, nrad, nlat, nlon), f32),
                 pltpu.VMEM((3, nrad, nlat, nlon), f32),
                 pltpu.VMEM((nrad, 3, nlat + 8, nlon), f32),
+                pltpu.VMEM((3, nrad, nlat, nlon), f32),
+                pltpu.VMEM((3, nrad, nlat, nlon), f32),
+                pltpu.VMEM((nrad, nlat, 2 * nlon), f32),
+                pltpu.VMEM((6 * nlon, 2 * nlon), jnp.bfloat16),
+                pltpu.VMEM((6 * nlon, nlon), jnp.bfloat16),
                 pltpu.VMEM((2, 2, nlat, nlon), f32),
-                pltpu.VMEM((2, 2, nlat, nlon), f32),
+                pltpu.VMEM((2, 2, 2, nlat, nlon), f32),
                 pltpu.VMEM((2, 2, 9 * nrad, nlon), f32),
                 pltpu.VMEM((2, 2, 9 * nrad, nlon), f32),
                 dma((8,)),

time: 38 us -> 32.8 us (0.86)
  Pallas kernels: 37.2 us -> 32 us
    pallas_call x1, Pallas kernels: 36.3 us -> 31.1 us  [shards(): pl.pallas_call(lambda *refs: kernel(nrad, nlat, nlon, counts, *refs), out...]
where the time goes in v3:
time: 32.8 us; the launch traced here: 32.7 us
  Pallas kernels  32 us (98%)
  between operations  0.64 us (2%)
    pallas_call x1, Pallas kernels, shards(): pl.pallas_call(lambda *refs: kernel(nrad, nlat, nlon, counts, *refs), out...  31.1 us
    pallas_call x1, Pallas kernels, shards(): pl.pallas_call(write_out, out_shape=(jax.ShapeDtypeStruct(blocks[0].shape...  0.93 us

profile of v3, /device:TPU:14, one launch (start us, length us, event | category | flops | bytes accessed | tf_op | source)
XLA Modules:
  0.0 32.7 jit_solution(7260151825547212572)
XLA Ops:
  0.6 31.1 %steps.1 = (f32[8,32,128]{2,1,0:T(8,128)S(1)}, f32[8,32,128]{2,1,0:T(8,128)S(1)}, f32[8,32,128]{2,1,0:T(8,128)S(1)}, f32[8,32,128]{2,1,0:T(8,128)S(1)}, f32[8,32...) custom-call(f32[8,32,128]{2,1,0:T(8,128)} %refs_0_.1, f32[8,32,128]{2,1,0:T(8,128)} %refs_1_.1, f32[8,32,128]{2,1,0:T(8,128)} %refs_2_.1, ...), custom_call_target="tpu_custom_call" | custom-call | tf_op jit(solution)/shard_map/steps/pallas_call | solution.py:354
  31.8 0.9 %write_out.1 = (f32[8,32,128]{2,1,0:T(8,128)}, f32[8,32,128]{2,1,0:T(8,128)}, f32[8,32,128]{2,1,0:T(8,128)}, f32[8,32,128]{2,1,0:T(8,128)}, f32[8,32,128]{2,1,0:T(8,128)}, /*index=5*/f32[8,32,128]{2,1,0:T(8,128)}) custom-call(f32[8,32,128]{2,1,0:T(8,128)S(1)} %get-tuple-element.12.refs_0_, f32[8,32,128]{2,1,0:T(8,128)S(1)} %get-tuple-element.13.refs_1_, ...), custom_call_target="tpu_custom_call" | custom-call | tf_op jit(solution)/shard_map/write_out/pallas_call | solution.py:380

commit v4 on v0

v4 whole, which is shorter than its diff:
```python
import jax
import jax.numpy as jnp
from jax import lax
from jax.experimental import pallas as pl
from jax.experimental.pallas import tpu as pltpu
from jax.sharding import PartitionSpec as P

MESH = pl.DeviceIdType.MESH

near = 9.0 / 8.0
far = -1.0 / 24.0
half_near = near / 2
half_far = far / 2

LAYER = 6
ROW = 8


def kernel(
    nrad, nlat, nlon, counts,
    adj_now, adj_next, fwd_now, fwd_next, stiffness, buoyancy, bulk_in, density_in,
    out_adj_now, out_adj_next, out_fwd_now, out_fwd_next, out_bulk, out_density,
    now, new, bulk, density, total, total_h, flux, lap, both, bands, bands_in,
    lon_send, lon_recv, cross_recv, diag_recv,
    load_sem, lon_ssem, lon_rsem, cross_ssem, cross_rsem, diag_ssem, diag_rsem,
    lat_ssem, lat_rsem, edge_ssem, edge_rsem, rad_ssem, rad_rsem,
):
    lons, lats, _ = counts
    lon = lax.axis_index("lon")
    lat = lax.axis_index("lat")
    core = lax.axis_index("rad")
    sides = (lax.rem(lon + 1, lons), lax.rem(lon + lons - 1, lons))
    other = 1 - core
    has_south = lat > 0
    has_north = lat < lats - 1
    ring = 2 * nlon
    x_half, h_half = pl.ds(0, nlon), pl.ds(nlon, nlon)
    layers, rows = pl.ds(LAYER, nrad), pl.ds(ROW, nlat)

    barrier = pltpu.get_barrier_semaphore()

    def greet(where):
        pl.semaphore_signal(barrier, inc=1, device_id=where, device_id_type=MESH)

    greet({"rad": other})
    for side in sides:
        greet({"lon": side})
        greet({"lon": side, "rad": other})
    for exists, to in ((has_south, lat - 1), (has_north, lat + 1)):

        @pl.when(exists)
        def _():
            greet({"lat": to})
            greet({"lat": to, "rad": other})
            for side in sides:
                greet({"lat": to, "lon": side})

    sources = (adj_now, fwd_now, buoyancy, stiffness, adj_next, fwd_next, bulk_in, density_in)
    targets = tuple(now.at[f, layers, rows, x_half] for f in range(6)) + (bulk, density)
    loads = []
    for k in range(8):
        loads.append(pltpu.make_async_copy(sources[k], targets[k], load_sem.at[k]))
        loads[-1].start()

    outside = pl.ds(3 + 11 * core, 3)
    for f in range(3):
        now[f, outside] = jnp.zeros((3,) + now.shape[2:], jnp.float32)
    for f in range(2):
        new[f, outside, rows, x_half] = jnp.zeros((3, nlat, nlon), jnp.float32)
    for d, exists in enumerate((has_south, has_north)):

        @pl.when(jnp.logical_not(exists))
        def _():
            diag_recv[d] = jnp.zeros(diag_recv.shape[1:], jnp.float32)
            beyond = pl.ds((ROW + nlat) * d, 8)
            for f in range(6):
                now[f, layers, beyond, x_half] = jnp.zeros((nrad, 8, nlon), jnp.float32)
                if f < 3:
                    joint = pl.ds(14 - 11 * core, 3)
                    now[f, joint, beyond, x_half] = jnp.zeros((3, 8, nlon), jnp.float32)

    def banded(columns, start):
        source = lax.broadcasted_iota(jnp.int32, (ring, columns), 0)
        place = lax.broadcasted_iota(jnp.int32, (ring, columns), 1)
        gap = lax.bitwise_and(source - place - start + ring, ring - 1)
        out = jnp.where(gap == 1, 27.0, 0.0) - jnp.where(gap == 0, 27.0, 0.0)
        out = out - jnp.where(gap == 2, 1.0, 0.0) + jnp.where(gap == ring - 1, 1.0, 0.0)
        return out.astype(jnp.bfloat16)

    for k in range(3):
        bands[pl.ds(ring * k, ring)] = banded(ring, 0)
        bands_in[pl.ds(ring * k, ring)] = banded(ring, -1)

    def layer_of(j):
        return LAYER + 7 - j + core * (2 * j - 7)

    def joint_layer(j):
        return 14 + j - core * (9 + 2 * j)

    parts = ([], [])
    for f in range(3):
        for j in range(3):
            parts[0].append((f, j, 6 * len(parts[0]), 6))
    for f in range(2):
        for j in range(3, nrad):
            parts[0].append((f, j, 6 * len(parts[0]), 6))
    for j in range(3, nrad):
        parts[1].append((2, j, 6 * len(parts[1]), 6))
    for f in range(3, 6):
        for j in range(nrad):
            parts[1].append((f, j, 36 + 3 * (len(parts[1]) - 5), 3))
    lane = lax.broadcasted_iota(jnp.int32, (nlat, nlon), 1)
    lane8 = lax.broadcasted_iota(jnp.int32, (8, nlon), 1)

    def pack():
        for part in range(2):
            to_east = jnp.zeros((nlat, nlon), jnp.float32)
            to_west = jnp.zeros((nlat, nlon), jnp.float32)
            for f, j, s, w in parts[part]:
                turned = pltpu.roll(now[f, layer_of(j), rows, x_half], (s + w - 128) % 128, 1)
                to_east = jnp.where((lane >= s) & (lane < s + w), turned, to_east)
                to_west = jnp.where((lane >= s + w) & (lane < s + 2 * w), turned, to_west)
            lon_send[0, part] = to_east
            lon_send[1, part] = to_west

    def unpack():
        for part in range(2):
            for f, j, s, w in parts[part]:
                at = layer_of(j)
                back = (128 - s - w) % 128
                edges = jnp.where(lane < s + w, lon_recv[0, part], lon_recv[1, part])
                now[f, at, rows, h_half] = pltpu.roll(edges, back, 1)
                if f < 3:
                    for d in range(2):
                        corner = jnp.where(
                            lane8 < s + w, diag_recv[d, 0, part], diag_recv[d, 1, part]
                        )
                        now[f, at, pl.ds((ROW + nlat) * d, 8), h_half] = pltpu.roll(corner, back, 1)
                    if j < 3:
                        edges = jnp.where(lane < s + w, cross_recv[0], cross_recv[1])
                        now[f, joint_layer(j), rows, h_half] = pltpu.roll(edges, back, 1)

    def remote(src, dst, ssem, rsem, where):
        return pltpu.make_async_remote_copy(
            src, dst, ssem, rsem, device_id=where, device_id_type=MESH
        )

    def lon_copy(way, side):
        return remote(
            lon_send.at[way], lon_recv.at[way], lon_ssem.at[way], lon_rsem.at[way], {"lon": side}
        )

    def cross_copy(way, side):
        return remote(
            lon_send.at[way, 0], cross_recv.at[way], cross_ssem.at[way], cross_rsem.at[way],
            {"lon": side, "rad": other},
        )

    def diag_copy(d, way, to, side):
        return remote(
            lon_send.at[way, :, pl.ds((nlat - 8) * (1 - d), 8)], diag_recv.at[d, way],
            diag_ssem.at[d, way], diag_rsem.at[d, way], {"lat": to, "lon": side},
        )

    def lat_copy(d, to):
        return remote(
            now.at[:, layers, pl.ds(ROW + (nlat - 8) * (1 - d), 8), x_half],
            now.at[:, layers, pl.ds((ROW + nlat) * d, 8), x_half],
            lat_ssem.at[d], lat_rsem.at[d], {"lat": to},
        )

    def edge_copy(d, to):
        return remote(
            now.at[pl.ds(0, 3), pl.ds(11 - 5 * core, 3), pl.ds(ROW + (nlat - 8) * (1 - d), 8), x_half],
            now.at[pl.ds(0, 3), pl.ds(3 + 11 * core, 3), pl.ds((ROW + nlat) * d, 8), x_half],
            edge_ssem.at[d], edge_rsem.at[d], {"lat": to, "rad": other},
        )

    def rad_copies():
        return (
            remote(
                now.at[pl.ds(0, 3), pl.ds(8 - 2 * core, 6), rows, x_half],
                now.at[pl.ds(0, 3), pl.ds(14 * core, 6), rows, x_half],
                rad_ssem.at[0], rad_rsem.at[0], {"rad": other},
            ),
            remote(
                now.at[pl.ds(3, 3), pl.ds(11 - 5 * core, 3), rows, x_half],
                now.at[pl.ds(3, 3), pl.ds(3 + 11 * core, 3), rows, x_half],
                rad_ssem.at[1], rad_rsem.at[1], {"rad": other},
            ),
        )

    goes = ((has_north, lat + 1), (has_south, lat - 1))
    comes = ((has_south, lat - 1), (has_north, lat + 1))

    def each_lat(pairs, act):
        for d, (exists, to) in enumerate(pairs):

            @pl.when(exists)
            def _():
                act(d, to)

    def send_diag(d, to):
        for way in range(2):
            diag_copy(d, way, to, sides[way]).start()

    def send_lat(d, to):
        edge_copy(d, to).start()
        lat_copy(d, to).start()

    def wait_lat(d, to):
        edge_copy(d, to).wait_recv()
        lat_copy(d, to).wait_recv()

    def wait_diag(d, to):
        for way in range(2):
            diag_copy(d, way, to, sides[1 - way]).wait_recv()

    def wait_sent_lat(d, to):
        edge_copy(d, to).wait_send()
        lat_copy(d, to).wait_send()
        for way in range(2):
            diag_copy(d, way, to, sides[way]).wait_send()

    def along_rad(source, low, n, row, tiles, lanes, into):
        for t in range(tiles):
            here = pl.ds(row + 8 * t, 8)
            adj, fwd = (source[f, pl.ds(low, n + 6), here, lanes] for f in range(2))
            buoy = now[2, pl.ds(low, n + 6), here, lanes]

            def faces(p):
                return near * (p[2 : n + 5] - p[1 : n + 4]) + far * (p[3 : n + 6] - p[0 : n + 3])

            weight = buoy[1 : n + 4] + buoy[2 : n + 5]
            grad_fwd = faces(fwd)
            flux_adj, flux_fwd = weight * faces(adj), weight * grad_fwd
            product = flux_adj * grad_fwd

            def diverge(q):
                return half_near * (q[2 : n + 2] - q[1 : n + 1]) + half_far * (
                    q[3 : n + 3] - q[0:n]
                )

            place = (pl.ds(0, n), pl.ds(8 * t, 8))
            into[(0,) + place] = diverge(flux_adj)
            into[(1,) + place] = diverge(flux_fwd)
            into[(2,) + place] = product[1 : n + 1] + product[2 : n + 2]

    def along_lat(source, low, n, row, count, lanes, into):
        for r in range(n):
            def at(ref, f, k):
                return ref[f, low + r, pl.ds(row - 2 + k, count + 8), lanes]

            def faces(f):
                return near * (at(source, f, 1) - at(source, f, 0)) + far * (
                    at(source, f, 2) - at(source, f, -1)
                )

            weight = at(now, 2, 0) + at(now, 2, 1)
            grad_fwd = faces(1)
            flux_adj = weight * faces(0)
            span = pl.ds(0, count + 8)
            flux[r, 0, span] = flux_adj
            flux[r, 1, span] = weight * grad_fwd
            flux[r, 2, span] = flux_adj * grad_fwd

            def moved(f, k):
                return flux[r, f, pl.ds(2 + k, count)]

            here = pl.ds(0, count)
            for f in range(2):
                into[f, r, here] += half_near * (moved(f, 0) - moved(f, -1)) + half_far * (
                    moved(f, 1) - moved(f, -2)
                )
            into[2, r, here] += moved(2, 0) + moved(2, -1)

    def times(x, matrix):
        cuts = []
        for k in range(3):
            cuts.append(x.astype(jnp.bfloat16))
            if k < 2:
                x = x - cuts[-1].astype(jnp.float32)
        return jnp.dot(
            jnp.concatenate(cuts, axis=1), matrix, preferred_element_type=jnp.float32
        )

    def set_both(low, n, row, count):
        lanes = lax.broadcasted_iota(jnp.int32, (count, nlon), 1)
        for r in range(n):
            here, past = (now[2, low + r, pl.ds(row, count), half] for half in (x_half, h_half))
            mixed = (jnp.where(lanes < 1, past, here), jnp.where(lanes < 1, here, past))
            both[r, :, x_half] = here + pltpu.roll(mixed[0], 127, 1)
            both[r, :, h_half] = past + pltpu.roll(mixed[1], 127, 1)

    def along_lon(source, low, n, row, count, weight, columns):
        cells = n * count
        slopes, fluxes = [], []
        for f in range(2):
            x = source[f, pl.ds(low, n), pl.ds(row, count)].reshape(cells, ring)
            slope = times(x, bands[...])
            q = weight * slope
            done = times(q, bands_in[:, pl.ds(0, columns)])
            lap[f, pl.ds(0, n), pl.ds(0, count), pl.ds(0, columns)] = done.reshape(n, count, columns)
            slopes.append(slope)
            fluxes.append(q)
        lap[2, pl.ds(0, n), pl.ds(0, count)] = (fluxes[0] * slopes[1]).reshape(n, count, ring)

    def density_along_lon(r, first_row):
        here, past = (lap[2, r, pl.ds(first_row, nlat), half] for half in (x_half, h_half))
        return here + pltpu.roll(jnp.where(lane >= 127, past, here), 1, 1)

    for k in range(6):
        loads[k].wait()
    pack()
    lat_count = has_south.astype(jnp.int32) + has_north.astype(jnp.int32)
    pl.semaphore_wait(barrier, 5 + 4 * lat_count)
    for way in range(2):
        lon_copy(way, sides[way]).start()
    for way in range(2):
        cross_copy(way, sides[way]).start()
    each_lat(goes, send_diag)
    for copy in rad_copies():
        copy.start()
    each_lat(goes, send_lat)
    loads[6].wait()
    loads[7].wait()

    base = LAYER - 3 * core
    extra = nrad + 3
    top, tall = ROW - 3, nlat + 8
    for copy in rad_copies():
        copy.wait_recv()
    each_lat(comes, wait_lat)
    along_rad(now, base - 3, extra, top, tall // 8, x_half, total)
    along_lat(now, base, extra, top, tall, x_half, total)
    for way in range(2):
        lon_copy(way, sides[1 - way]).wait_recv()
        cross_copy(way, sides[1 - way]).wait_recv()
    each_lat(comes, wait_diag)
    unpack()
    along_rad(now, LAYER - 3, nrad, ROW, nlat // 8, h_half, total_h)
    along_lat(now, LAYER, nrad, ROW, nlat, h_half, total_h)
    set_both(base, extra, top, tall)
    along_lon(now, base, extra, top, tall, both[...].reshape(extra * tall, ring), ring)

    own = 3 * core

    def advance(f, at, here, half, sums, lap_at):
        slope = now[3, at, here, half] * (sums + (1 / 1152) * lap_at)
        fresh = 2.0 * now[f, at, here, half] - now[4 + f, at, here, half] + slope
        return fresh, slope

    for r in range(extra):
        here = pl.ds(top, tall)
        for f in range(2):
            fresh, _ = advance(f, base + r, here, x_half, total[f, r], lap[f, r, :, x_half])
            new[f, base + r, here, x_half] = fresh
    mine = pl.ds(3, nlat)
    for r in range(nrad):
        for f in range(2):
            fresh, _ = advance(
                f, LAYER + r, rows, h_half, total_h[f, r], lap[f, own + r, mine, h_half]
            )
            new[f, LAYER + r, rows, h_half] = fresh
        slope = now[3, LAYER + r, rows, x_half] * (
            total[1, own + r, mine] + (1 / 1152) * lap[1, own + r, mine, x_half]
        )
        bulk[r] += now[0, LAYER + r, rows, x_half] * slope
        density[r] += 0.25 * total[2, own + r, mine] + (1 / 2304) * density_along_lon(own + r, 3)
        out_adj_next[r] = new[0, LAYER + r, rows, x_half]
        out_fwd_next[r] = new[1, LAYER + r, rows, x_half]

    along_rad(new, LAYER - 3, nrad, ROW, nlat // 8, x_half, total)
    along_lat(new, LAYER, nrad, ROW, nlat, x_half, total)
    weight = both[pl.ds(own, nrad), mine].reshape(nrad * nlat, ring)
    along_lon(new, LAYER, nrad, ROW, nlat, weight, nlon)
    first_rows = pl.ds(0, nlat)
    for r in range(nrad):
        adj, fwd = new[0, LAYER + r, rows, x_half], new[1, LAYER + r, rows, x_half]
        stiff = now[3, LAYER + r, rows, x_half]
        lap_adj = stiff * (total[0, r, first_rows] + (1 / 1152) * lap[0, r, first_rows, x_half])
        lap_fwd = stiff * (total[1, r, first_rows] + (1 / 1152) * lap[1, r, first_rows, x_half])
        out_bulk[r] = bulk[r] + adj * lap_fwd
        out_density[r] = density[r] + (
            0.25 * total[2, r, first_rows] + (1 / 2304) * density_along_lon(r, 0)
        )
        out_adj_now[r] = 2.0 * adj - now[0, LAYER + r, rows, x_half] + lap_adj
        out_fwd_now[r] = 2.0 * fwd - now[1, LAYER + r, rows, x_half] + lap_fwd

    for way in range(2):
        lon_copy(way, sides[way]).wait_send()
        cross_copy(way, sides[way]).wait_send()
    each_lat(goes, wait_sent_lat)
    for copy in rad_copies():
        copy.wait_send()


def write_out(*refs):
    results, outs, sems = refs[:6], refs[6:12], refs[12]
    copies = [
        pltpu.make_async_copy(result, out, sems.at[k])
        for k, (result, out) in enumerate(zip(results, outs))
    ]
    for copy in copies:
        copy.start()
    for copy in copies:
        copy.wait()


def solution(mesh):
    counts = (mesh.shape["lon"], mesh.shape["lat"], mesh.shape["rad"])

    def shards(*blocks):
        nrad, nlat, nlon = blocks[0].shape
        f32, dma, vmem = jnp.float32, pltpu.SemaphoreType.DMA, pltpu.VMEM
        depth, tall, ring = nrad + 12, nlat + 24, 2 * nlon
        held = pl.pallas_call(
            lambda *refs: kernel(nrad, nlat, nlon, counts, *refs),
            out_shape=(vmem(blocks[0].shape, f32),) * 6,
            in_specs=[pl.BlockSpec(memory_space=pl.ANY)] * 8,
            out_specs=(pl.BlockSpec(memory_space=vmem),) * 6,
            scratch_shapes=[
                vmem((6, depth, tall, ring), f32),
                vmem((2, depth, tall, ring), f32),
                vmem((nrad, nlat, nlon), f32),
                vmem((nrad, nlat, nlon), f32),
                vmem((3, nrad + 3, nlat + 8, nlon), f32),
                vmem((3, nrad, nlat, nlon), f32),
                vmem((nrad + 3, 3, nlat + 16, nlon), f32),
                vmem((3, nrad + 3, nlat + 8, ring), f32),
                vmem((nrad + 3, nlat + 8, ring), f32),
                vmem((3 * ring, ring), jnp.bfloat16),
                vmem((3 * ring, ring), jnp.bfloat16),
                vmem((2, 2, nlat, nlon), f32),
                vmem((2, 2, nlat, nlon), f32),
                vmem((2, nlat, nlon), f32),
                vmem((2, 2, 2, 8, nlon), f32),
                dma((8,)), dma((2,)), dma((2,)), dma((2,)), dma((2,)), dma((2, 2)), dma((2, 2)),
                dma((2,)), dma((2,)), dma((2,)), dma((2,)), dma((2,)), dma((2,)),
            ],
            compiler_params=pltpu.CompilerParams(collective_id=0, has_side_effects=True),
            name="steps",
        )(*blocks)
        held = tuple(pltpu.with_memory_space_constraint(x, vmem) for x in held)
        return pl.pallas_call(
            write_out,
            out_shape=(jax.ShapeDtypeStruct(blocks[0].shape, f32),) * 6,
            in_specs=[pl.BlockSpec(memory_space=vmem)] * 6,
            out_specs=(pl.BlockSpec(memory_space=pl.ANY),) * 6,
            scratch_shapes=[dma((6,))],
            name="write_out",
        )(*held)

    spec = P("rad", "lat", "lon")
    return jax.shard_map(
        shards, mesh=mesh, in_specs=(spec,) * 8, out_specs=(spec,) * 6, check_vma=False
    )
```

time: 108 us -> 34.5 us (0.32)
  the two profiles are of different devices: /device:TPU:7 before, /device:TPU:14 now
where the time goes in v4:
time: 34.5 us; the launch traced here: 34.3 us
  Pallas kernels  33.7 us (98%)
  between operations  0.64 us (2%)
    pallas_call x1, Pallas kernels, shards(): pl.pallas_call(lambda *refs: kernel(nrad, nlat, nlon, counts, *refs), out...  32.7 us
    pallas_call x1, Pallas kernels, shards(): pl.pallas_call(write_out, out_shape=(jax.ShapeDtypeStruct(blocks[0].shape...  0.93 us

profile of v4, /device:TPU:14, one launch (start us, length us, event | category | flops | bytes accessed | tf_op | source)
XLA Modules:
  0.0 34.3 jit_solution(1094917008526634351)
XLA Ops:
  0.6 32.7 %steps.1 = (f32[8,32,128]{2,1,0:T(8,128)S(1)}, f32[8,32,128]{2,1,0:T(8,128)S(1)}, f32[8,32,128]{2,1,0:T(8,128)S(1)}, f32[8,32,128]{2,1,0:T(8,128)S(1)}, f32[8,32...) custom-call(f32[8,32,128]{2,1,0:T(8,128)} %refs_0_.1, f32[8,32,128]{2,1,0:T(8,128)} %refs_1_.1, f32[8,32,128]{2,1,0:T(8,128)} %refs_2_.1, ...), custom_call_target="tpu_custom_call" | custom-call | tf_op jit(solution)/shard_map/steps/pallas_call | solution.py:417
  33.4 0.9 %write_out.1 = (f32[8,32,128]{2,1,0:T(8,128)}, f32[8,32,128]{2,1,0:T(8,128)}, f32[8,32,128]{2,1,0:T(8,128)}, f32[8,32,128]{2,1,0:T(8,128)}, f32[8,32,128]{2,1,0:T(8,128)}, /*index=5*/f32[8,32,128]{2,1,0:T(8,128)}) custom-call(f32[8,32,128]{2,1,0:T(8,128)S(1)} %get-tuple-element.12.refs_0_, f32[8,32,128]{2,1,0:T(8,128)S(1)} %get-tuple-element.13.refs_1_, ...), custom_call_target="tpu_custom_call" | custom-call | tf_op jit(solution)/shard_map/write_out/pallas_call | solution.py:445

commit v5 on v4

--- a/solution.py
+++ b/solution.py
@@ -21,7 +21,7 @@
     adj_now, adj_next, fwd_now, fwd_next, stiffness, buoyancy, bulk_in, density_in,
     out_adj_now, out_adj_next, out_fwd_now, out_fwd_next, out_bulk, out_density,
     now, new, bulk, density, total, total_h, flux, lap, both, bands, bands_in,
-    lon_send, lon_recv, cross_recv, diag_recv,
+    lon_send, lon_recv, cross_recv, diag_recv, lat_send, lat_recv, edge_recv,
     load_sem, lon_ssem, lon_rsem, cross_ssem, cross_rsem, diag_ssem, diag_rsem,
     lat_ssem, lat_rsem, edge_ssem, edge_rsem, rad_ssem, rad_rsem,
 ):
@@ -72,12 +72,8 @@
         @pl.when(jnp.logical_not(exists))
         def _():
             diag_recv[d] = jnp.zeros(diag_recv.shape[1:], jnp.float32)
-            beyond = pl.ds((ROW + nlat) * d, 8)
-            for f in range(6):
-                now[f, layers, beyond, x_half] = jnp.zeros((nrad, 8, nlon), jnp.float32)
-                if f < 3:
-                    joint = pl.ds(14 - 11 * core, 3)
-                    now[f, joint, beyond, x_half] = jnp.zeros((3, 8, nlon), jnp.float32)
+            lat_recv[d] = jnp.zeros(lat_recv.shape[1:], jnp.float32)
+            edge_recv[d] = jnp.zeros(edge_recv.shape[1:], jnp.float32)
 
     def banded(columns, start):
         source = lax.broadcasted_iota(jnp.int32, (ring, columns), 0)
@@ -122,6 +118,25 @@
                 to_west = jnp.where((lane >= s + w) & (lane < s + 2 * w), turned, to_west)
             lon_send[0, part] = to_east
             lon_send[1, part] = to_west
+
+    lines = []
+    for depth, group in ((0, range(3)), (3, range(3)), (0, range(3, 6))):
+        for j in range(nrad):
+            for f in group:
+                lines.append((f, j, depth, pl.ds(3 * len(lines), 3)))
+
+    def pack_rows():
+        for f, j, depth, line in lines:
+            at = layer_of(j)
+            lat_send[0, line] = now[f, at, pl.ds(ROW + nlat - 3 - depth, 3), x_half]
+            lat_send[1, line] = now[f, at, pl.ds(ROW + depth, 3), x_half]
+
+    def unpack_rows():
+        for k, (f, j, depth, line) in enumerate(lines):
+            for d, row in enumerate((ROW - 3 - depth, ROW + nlat + depth)):
+                now[f, layer_of(j), pl.ds(row, 3), x_half] = lat_recv[d, line]
+                if k < 9:
+                    now[f, joint_layer(j), pl.ds(row, 3), x_half] = edge_recv[d, line]
 
     def unpack():
         for part in range(2):
@@ -164,16 +179,13 @@
 
     def lat_copy(d, to):
         return remote(
-            now.at[:, layers, pl.ds(ROW + (nlat - 8) * (1 - d), 8), x_half],
-            now.at[:, layers, pl.ds((ROW + nlat) * d, 8), x_half],
-            lat_ssem.at[d], lat_rsem.at[d], {"lat": to},
+            lat_send.at[d], lat_recv.at[d], lat_ssem.at[d], lat_rsem.at[d], {"lat": to}
         )
 
     def edge_copy(d, to):
         return remote(
-            now.at[pl.ds(0, 3), pl.ds(11 - 5 * core, 3), pl.ds(ROW + (nlat - 8) * (1 - d), 8), x_half],
-            now.at[pl.ds(0, 3), pl.ds(3 + 11 * core, 3), pl.ds((ROW + nlat) * d, 8), x_half],
-            edge_ssem.at[d], edge_rsem.at[d], {"lat": to, "rad": other},
+            lat_send.at[d, pl.ds(0, 32)], edge_recv.at[d], edge_ssem.at[d], edge_rsem.at[d],
+            {"lat": to, "rad": other},
         )
 
     def rad_copies():
@@ -205,8 +217,8 @@
             diag_copy(d, way, to, sides[way]).start()
 
     def send_lat(d, to):
+        lat_copy(d, to).start()
         edge_copy(d, to).start()
-        lat_copy(d, to).start()
 
     def wait_lat(d, to):
         edge_copy(d, to).wait_recv()
@@ -222,9 +234,9 @@
         for way in range(2):
             diag_copy(d, way, to, sides[way]).wait_send()
 
-    def along_rad(source, low, n, row, tiles, lanes, into):
-        for t in range(tiles):
-            here = pl.ds(row + 8 * t, 8)
+    def along_rad(source, low, n, starts, lanes, into, skip, drop):
+        for start in starts:
+            here = pl.ds(start, 8)
             adj, fwd = (source[f, pl.ds(low, n + 6), here, lanes] for f in range(2))
             buoy = now[2, pl.ds(low, n + 6), here, lanes]
 
@@ -241,12 +253,12 @@
                     q[3 : n + 3] - q[0:n]
                 )
 
-            place = (pl.ds(0, n), pl.ds(8 * t, 8))
+            place = (pl.ds(skip, n), pl.ds(start - drop, 8))
             into[(0,) + place] = diverge(flux_adj)
             into[(1,) + place] = diverge(flux_fwd)
             into[(2,) + place] = product[1 : n + 1] + product[2 : n + 2]
 
-    def along_lat(source, low, n, row, count, lanes, into):
+    def along_lat(source, low, n, row, count, lanes, into, put):
         for r in range(n):
             def at(ref, f, k):
                 return ref[f, low + r, pl.ds(row - 2 + k, count + 8), lanes]
@@ -267,7 +279,7 @@
             def moved(f, k):
                 return flux[r, f, pl.ds(2 + k, count)]
 
-            here = pl.ds(0, count)
+            here = pl.ds(put, count)
             for f in range(2):
                 into[f, r, here] += half_near * (moved(f, 0) - moved(f, -1)) + half_far * (
                     moved(f, 1) - moved(f, -2)
@@ -312,6 +324,7 @@
     for k in range(6):
         loads[k].wait()
     pack()
+    pack_rows()
     lat_count = has_south.astype(jnp.int32) + has_north.astype(jnp.int32)
     pl.semaphore_wait(barrier, 5 + 4 * lat_count)
     for way in range(2):
@@ -319,31 +332,32 @@
     for way in range(2):
         cross_copy(way, sides[way]).start()
     each_lat(goes, send_diag)
+    each_lat(goes, send_lat)
     for copy in rad_copies():
         copy.start()
-    each_lat(goes, send_lat)
     loads[6].wait()
     loads[7].wait()
 
     base = LAYER - 3 * core
     extra = nrad + 3
     top, tall = ROW - 3, nlat + 8
+    own = 3 * core
     for copy in rad_copies():
         copy.wait_recv()
+    along_rad(now, base - 3, extra, range(ROW, ROW + nlat, 8), x_half, total, 0, 0)
     each_lat(comes, wait_lat)
-    along_rad(now, base - 3, extra, top, tall // 8, x_half, total)
-    along_lat(now, base, extra, top, tall, x_half, total)
+    unpack_rows()
+    along_rad(now, LAYER - 3, nrad, (0, ROW + nlat), x_half, total, own, 0)
+    along_lat(now, base, extra, top, tall, x_half, total, top)
     for way in range(2):
         lon_copy(way, sides[1 - way]).wait_recv()
         cross_copy(way, sides[1 - way]).wait_recv()
     each_lat(comes, wait_diag)
     unpack()
-    along_rad(now, LAYER - 3, nrad, ROW, nlat // 8, h_half, total_h)
-    along_lat(now, LAYER, nrad, ROW, nlat, h_half, total_h)
+    along_rad(now, LAYER - 3, nrad, range(ROW, ROW + nlat, 8), h_half, total_h, 0, ROW)
+    along_lat(now, LAYER, nrad, ROW, nlat, h_half, total_h, 0)
     set_both(base, extra, top, tall)
     along_lon(now, base, extra, top, tall, both[...].reshape(extra * tall, ring), ring)
-
-    own = 3 * core
 
     def advance(f, at, here, half, sums, lap_at):
         slope = now[3, at, here, half] * (sums + (1 / 1152) * lap_at)
@@ -353,7 +367,7 @@
     for r in range(extra):
         here = pl.ds(top, tall)
         for f in range(2):
-            fresh, _ = advance(f, base + r, here, x_half, total[f, r], lap[f, r, :, x_half])
+            fresh, _ = advance(f, base + r, here, x_half, total[f, r, here], lap[f, r, :, x_half])
             new[f, base + r, here, x_half] = fresh
     mine = pl.ds(3, nlat)
     for r in range(nrad):
@@ -363,15 +377,15 @@
             )
             new[f, LAYER + r, rows, h_half] = fresh
         slope = now[3, LAYER + r, rows, x_half] * (
-            total[1, own + r, mine] + (1 / 1152) * lap[1, own + r, mine, x_half]
+            total[1, own + r, rows] + (1 / 1152) * lap[1, own + r, mine, x_half]
         )
         bulk[r] += now[0, LAYER + r, rows, x_half] * slope
-        density[r] += 0.25 * total[2, own + r, mine] + (1 / 2304) * density_along_lon(own + r, 3)
+        density[r] += 0.25 * total[2, own + r, rows] + (1 / 2304) * density_along_lon(own + r, 3)
         out_adj_next[r] = new[0, LAYER + r, rows, x_half]
         out_fwd_next[r] = new[1, LAYER + r, rows, x_half]
 
-    along_rad(new, LAYER - 3, nrad, ROW, nlat // 8, x_half, total)
-    along_lat(new, LAYER, nrad, ROW, nlat, x_half, total)
+    along_rad(new, LAYER - 3, nrad, range(ROW, ROW + nlat, 8), x_half, total, 0, ROW)
+    along_lat(new, LAYER, nrad, ROW, nlat, x_half, total, 0)
     weight = both[pl.ds(own, nrad), mine].reshape(nrad * nlat, ring)
     along_lon(new, LAYER, nrad, ROW, nlat, weight, nlon)
     first_rows = pl.ds(0, nlat)
@@ -424,7 +438,7 @@
                 vmem((2, depth, tall, ring), f32),
                 vmem((nrad, nlat, nlon), f32),
                 vmem((nrad, nlat, nlon), f32),
-                vmem((3, nrad + 3, nlat + 8, nlon), f32),
+                vmem((3, nrad + 3, nlat + 16, nlon), f32),
                 vmem((3, nrad, nlat, nlon), f32),
                 vmem((nrad + 3, 3, nlat + 16, nlon), f32),
                 vmem((3, nrad + 3, nlat + 8, ring), f32),
@@ -435,6 +449,9 @@
                 vmem((2, 2, nlat, nlon), f32),
                 vmem((2, nlat, nlon), f32),
                 vmem((2, 2, 2, 8, nlon), f32),
+                vmem((2, 27 * nrad, nlon), f32),
+                vmem((2, 27 * nrad, nlon), f32),
+                vmem((2, 32, nlon), f32),
                 dma((8,)), dma((2,)), dma((2,)), dma((2,)), dma((2,)), dma((2, 2)), dma((2, 2)),
                 dma((2,)), dma((2,)), dma((2,)), dma((2,)), dma((2,)), dma((2,)),
             ],

time: 34.5 us -> 32.1 us (0.930); the launches traced: 34.3 us -> 31.5 us
  Pallas kernels: 33.7 us -> 30.9 us
    pallas_call x1, Pallas kernels: 32.7 us -> 29.9 us  [shards(): pl.pallas_call(lambda *refs: kernel(nrad, nlat, nlon, counts, *refs), out...]
where the time goes in v5:
time: 32.1 us; the launch traced here: 31.5 us
  Pallas kernels  30.9 us (96%)
  between operations  0.64 us (2%)
    pallas_call x1, Pallas kernels, shards(): pl.pallas_call(lambda *refs: kernel(nrad, nlat, nlon, counts, *refs), out...  29.9 us
    pallas_call x1, Pallas kernels, shards(): pl.pallas_call(write_out, out_shape=(jax.ShapeDtypeStruct(blocks[0].shape...  0.93 us

profile of v5, /device:TPU:14, one launch (start us, length us, event | category | flops | bytes accessed | tf_op | source)
XLA Modules:
  0.0 31.5 jit_solution(1138734683424645145)
XLA Ops:
  0.6 29.9 %steps.1 = (f32[8,32,128]{2,1,0:T(8,128)S(1)}, f32[8,32,128]{2,1,0:T(8,128)S(1)}, f32[8,32,128]{2,1,0:T(8,128)S(1)}, f32[8,32,128]{2,1,0:T(8,128)S(1)}, f32[8,32...) custom-call(f32[8,32,128]{2,1,0:T(8,128)} %refs_0_.1, f32[8,32,128]{2,1,0:T(8,128)} %refs_1_.1, f32[8,32,128]{2,1,0:T(8,128)} %refs_2_.1, ...), custom_call_target="tpu_custom_call" | custom-call | tf_op jit(solution)/shard_map/steps/pallas_call | solution.py:431
  30.6 0.9 %write_out.1 = (f32[8,32,128]{2,1,0:T(8,128)}, f32[8,32,128]{2,1,0:T(8,128)}, f32[8,32,128]{2,1,0:T(8,128)}, f32[8,32,128]{2,1,0:T(8,128)}, f32[8,32,128]{2,1,0:T(8,128)}, /*index=5*/f32[8,32,128]{2,1,0:T(8,128)}) custom-call(f32[8,32,128]{2,1,0:T(8,128)S(1)} %get-tuple-element.12.refs_0_, f32[8,32,128]{2,1,0:T(8,128)S(1)} %get-tuple-element.13.refs_1_, ...), custom_call_target="tpu_custom_call" | custom-call | tf_op jit(solution)/shard_map/write_out/pallas_call | solution.py:462

commit v6 on v5

--- a/solution.py
+++ b/solution.py
@@ -345,10 +345,6 @@
     for copy in rad_copies():
         copy.wait_recv()
     along_rad(now, base - 3, extra, range(ROW, ROW + nlat, 8), x_half, total, 0, 0)
-    each_lat(comes, wait_lat)
-    unpack_rows()
-    along_rad(now, LAYER - 3, nrad, (0, ROW + nlat), x_half, total, own, 0)
-    along_lat(now, base, extra, top, tall, x_half, total, top)
     for way in range(2):
         lon_copy(way, sides[1 - way]).wait_recv()
         cross_copy(way, sides[1 - way]).wait_recv()
@@ -356,6 +352,10 @@
     unpack()
     along_rad(now, LAYER - 3, nrad, range(ROW, ROW + nlat, 8), h_half, total_h, 0, ROW)
     along_lat(now, LAYER, nrad, ROW, nlat, h_half, total_h, 0)
+    each_lat(comes, wait_lat)
+    unpack_rows()
+    along_rad(now, LAYER - 3, nrad, (0, ROW + nlat), x_half, total, own, 0)
+    along_lat(now, base, extra, top, tall, x_half, total, top)
     set_both(base, extra, top, tall)
     along_lon(now, base, extra, top, tall, both[...].reshape(extra * tall, ring), ring)
 

time: 32.1 us -> 31.6 us (0.984)
  the two profiles are of different devices: /device:TPU:14 before, /device:TPU:1 now
where the time goes in v6:
time: 31.6 us; the launch traced here: 31.5 us
  Pallas kernels  30.8 us (97%)
  between operations  0.64 us (2%)
    pallas_call x1, Pallas kernels, shards(): pl.pallas_call(lambda *refs: kernel(nrad, nlat, nlon, counts, *refs), out...  29.9 us
    pallas_call x1, Pallas kernels, shards(): pl.pallas_call(write_out, out_shape=(jax.ShapeDtypeStruct(blocks[0].shape...  0.93 us

profile of v6, /device:TPU:1, one launch (start us, length us, event | category | flops | bytes accessed | tf_op | source)
XLA Modules:
  0.0 31.5 jit_solution(8838601177122369827)
XLA Ops:
  0.6 29.9 %steps.1 = (f32[8,32,128]{2,1,0:T(8,128)S(1)}, f32[8,32,128]{2,1,0:T(8,128)S(1)}, f32[8,32,128]{2,1,0:T(8,128)S(1)}, f32[8,32,128]{2,1,0:T(8,128)S(1)}, f32[8,32...) custom-call(f32[8,32,128]{2,1,0:T(8,128)} %refs_0_.1, f32[8,32,128]{2,1,0:T(8,128)} %refs_1_.1, f32[8,32,128]{2,1,0:T(8,128)} %refs_2_.1, ...), custom_call_target="tpu_custom_call" | custom-call | tf_op jit(solution)/shard_map/steps/pallas_call | solution.py:431
  30.5 0.9 %write_out.1 = (f32[8,32,128]{2,1,0:T(8,128)}, f32[8,32,128]{2,1,0:T(8,128)}, f32[8,32,128]{2,1,0:T(8,128)}, f32[8,32,128]{2,1,0:T(8,128)}, f32[8,32,128]{2,1,0:T(8,128)}, /*index=5*/f32[8,32,128]{2,1,0:T(8,128)}) custom-call(f32[8,32,128]{2,1,0:T(8,128)S(1)} %get-tuple-element.12.refs_0_, f32[8,32,128]{2,1,0:T(8,128)S(1)} %get-tuple-element.13.refs_1_, ...), custom_call_target="tpu_custom_call" | custom-call | tf_op jit(solution)/shard_map/write_out/pallas_call | solution.py:462
